TPU v7x, 128 devices: a whole 4x4x4 slice. The times are simulated.
128 devices in a mesh: expert: 8 (over z_lo, x), shard: 16 (over z_hi, y, core).
Axes of the slice: x: 4, y: 4, z: 4 (z_hi: 2, z_lo: 2; z = z_hi * 2 + z_lo), core: 2. Of those that a mesh axis runs over, the one named last changes fastest.
Arguments:
- tokens: bfloat16 [1024, 4096], P('expert', 'shard'), may hold values from -6 to 6
- routes: int32 [1024, 2], P('expert'), may hold values from 0 to 7, all different within a row; in each aligned block of 128 rows (0 to 127, 128 to 255, ...) at most 96 rows name the same one
- mix_weights: float32 [1024, 2], P('expert'), may hold values from 0.1 to 1
- cotangent: bfloat16 [1024, 4096], P('expert', 'shard'), may hold values from -6 to 6
- w_gate: bfloat16 [8, 4096, 6144], P('expert', 'shard'), may hold values from -0.09375 to 0.09375
- w_up: bfloat16 [8, 4096, 6144], P('expert', 'shard'), may hold values from -0.09375 to 0.09375
- w_down: bfloat16 [8, 4096, 6144], P('expert', 'shard'), may hold values from -0.078125 to 0.078125
Outputs:
- layer_out: bfloat16 [1024, 4096], P('expert', 'shard')
- grad_tokens: bfloat16 [1024, 4096], P('expert', 'shard')
- grad_gate: bfloat16 [8, 4096, 6144], P('expert', None, 'shard')
- grad_up: bfloat16 [8, 4096, 6144], P('expert', None, 'shard')
- grad_down: bfloat16 [8, 4096, 6144], P('expert', None, 'shard')
Inputs may be any that keep to these rules, and one draw needn't show every extreme that they name: `routes`: each token names two different experts. Among the 128 tokens of one block, no expert is named by more than 96 tokens, and in every draw some expert is named by exactly 96 tokens of some block. Every expert is named by some token.
All inputs are finite; a program needn't handle non-finite values.
Results may differ from a plain program's by a relative error of at most 0.015.
Values may be sent and summed in bfloat16 or wider, within the bound.
No kernel may reach another device: no remote copies, remote signals or barrier semaphores. Data moves between devices by JAX's collectives and lax.ppermute only.
A program may use at most 128 MiB of HBM per device.

v0:
```python
import jax
import jax.numpy as jnp
from jax import lax
from jax.experimental import pallas as pl
from jax.experimental.pallas import tpu as pltpu
from jax.sharding import Mesh, PartitionSpec as P


EXPERT = ("z_lo", "x")
SHARD = ("z_hi", "y", "core")
N_X, N_CHIP = 4, 8


def swap(value, axes, size, offset):
    return lax.ppermute(value, axes, [(i, i ^ offset) for i in range(size)])


def chip_swap(value, k):
    return swap(value, ("z_hi", "y"), N_CHIP, k)


def core_swap(value):
    return swap(value, "core", 2, 1)


def dot(a, b, contract):
    return lax.dot_general(a, b, ((contract[0], contract[1]), ((), ())), preferred_element_type=jnp.float32)


def pack(weights, shard):
    rows, hidden = weights[0].shape
    piece = hidden // (2 * N_CHIP)
    step = rows // 2

    def kernel(shard_ref, *refs):
        ins, outs = refs[: len(weights)], refs[len(weights) :]
        chip, core = shard_ref[0] // 2, shard_ref[0] % 2
        for k, out in enumerate(outs):
            first = 2 * jnp.bitwise_xor(chip, k)
            for b, place in enumerate((first + core, first + 1 - core)):
                at = pl.ds(pl.multiple_of(place * piece, piece), piece)
                for n, ref in enumerate(ins):
                    to = (b * len(weights) + n) * piece
                    out[:, to : to + piece] = ref[:, at]

    width = 2 * piece * len(weights)
    return pl.pallas_call(
        kernel,
        grid_spec=pltpu.PrefetchScalarGridSpec(
            num_scalar_prefetch=1,
            grid=(rows // step,),
            in_specs=[pl.BlockSpec((step, hidden), lambda i, s: (i, 0)) for _ in weights],
            out_specs=[pl.BlockSpec((step, width), lambda i, s: (i, 0))] * N_CHIP,
        ),
        out_shape=[jax.ShapeDtypeStruct((rows, width), weights[0].dtype)] * N_CHIP,
        name="pack",
    )(shard, *weights)


def pack_natural(weight, shard):
    rows, hidden = weight.shape
    piece = hidden // (2 * N_CHIP)
    step = rows // 2

    def kernel(shard_ref, ref, out):
        core = shard_ref[0] % 2
        for chip in range(N_CHIP):
            for b, place in enumerate((2 * chip + core, 2 * chip + 1 - core)):
                at = pl.ds(pl.multiple_of(place * piece, piece), piece)
                out[chip, :, b * piece : (b + 1) * piece] = ref[:, at]

    return pl.pallas_call(
        kernel,
        grid_spec=pltpu.PrefetchScalarGridSpec(
            num_scalar_prefetch=1,
            grid=(rows // step,),
            in_specs=[pl.BlockSpec((step, hidden), lambda i, s: (i, 0))],
            out_specs=pl.BlockSpec((N_CHIP, step, 2 * piece), lambda i, s: (0, i, 0)),
        ),
        out_shape=jax.ShapeDtypeStruct((N_CHIP, rows, 2 * piece), weight.dtype),
        name="pack",
    )(shard, weight)


def chip_exchange(value):
    return lax.all_to_all(value, ("z_hi", "y"), split_axis=0, concat_axis=0, tiled=True)


def exchange(pieces):
    return [pieces[0]] + [chip_swap(pieces[k], k) for k in range(1, N_CHIP)]


def weight_grad(own, other, right, shard, n_out, natural):
    rows, half = own[0].shape
    piece = half // N_CHIP
    width = right.shape[1] // n_out

    def kernel(shard_ref, *refs):
        core = shard_ref[0] % 2
        right_ref, outs = refs[2 * N_X], refs[2 * N_X + 1 :]
        for ins, place in ((refs[:N_X], core), (refs[N_X : 2 * N_X], 1 - core)):
            left = jnp.concatenate([ref[...] for ref in ins], axis=0)
            total = dot(left, right_ref[...], ((0,), (0,))).astype(outs[0].dtype)
            at = pl.ds(pl.multiple_of(place * piece, piece), piece)
            for n, out in enumerate(outs):
                out[0, at, :] = total[:, n * width : (n + 1) * width]

    in_block = pl.BlockSpec((rows, piece), lambda k, s: (0, k))
    out_block = pl.BlockSpec((1, 2 * piece, width), lambda k, s: (0, k if natural else jnp.bitwise_xor(s[0] // 2, k), 0))
    return pl.pallas_call(
        kernel,
        grid_spec=pltpu.PrefetchScalarGridSpec(
            num_scalar_prefetch=1,
            grid=(N_CHIP,),
            in_specs=[in_block] * (2 * N_X) + [pl.BlockSpec(right.shape, lambda k, s: (0, 0))],
            out_specs=[out_block] * n_out,
        ),
        out_shape=[jax.ShapeDtypeStruct((1, 2 * half, width), jnp.bfloat16)] * n_out,
        cost_estimate=pl.CostEstimate(
            flops=4 * N_X * rows * half * right.shape[1],
            bytes_accessed=4 * N_X * rows * half + 2 * right.size + 4 * half * right.shape[1],
            transcendentals=0,
        ),
        name="weight_grad",
    )(shard, *own, *other, right)


def join(first, second, others):
    def kernel(first_ref, second_ref, others_ref, out):
        out[0, 0], out[0, 1] = first_ref[...], second_ref[...]
        out[1] = others_ref[...]

    shape = jax.ShapeDtypeStruct((2, *others.shape), others.dtype)
    return pl.pallas_call(kernel, out_shape=shape, name="join")(first, second, others)


def pick(pieces, which, place, mix, shard, capacity):
    tokens, piece = pieces[0].shape[2:]

    def kernel(shard_ref, place_ref, *refs):
        ins, outs = refs[:N_CHIP], refs[-N_X:]
        chip = shard_ref[0] // 2
        number = lax.broadcasted_iota(jnp.int32, (N_X * capacity, tokens), 0)
        for block in range(2):
            found = [number == place_ref[block, n : n + 1] for n in range(2)]
            picker = jnp.where(found[0] | found[1], 1.0, 0.0).astype(jnp.bfloat16)
            if mix is not None:
                shares = [jnp.where(f, refs[N_CHIP][block, n : n + 1], 0.0) for n, f in enumerate(found)]
                weight = jnp.sum(shares[0] + shares[1], axis=1, keepdims=True)
            for k, ref in enumerate(ins):
                rows = dot(picker, ref[block, which], ((1,), (0,)))
                to = k
                if mix is not None:
                    rows = rows * weight
                    to = jnp.bitwise_xor(chip, k)
                rows = rows.astype(jnp.bfloat16)
                columns = pl.ds(pl.multiple_of(to * piece, piece), piece)
                for d, out in enumerate(outs):
                    out[block * capacity : (block + 1) * capacity, columns] = rows[d * capacity : (d + 1) * capacity]

    extra = [] if mix is None else [mix]
    vmem = pl.BlockSpec(memory_space=pltpu.VMEM)
    return pl.pallas_call(
        kernel,
        in_specs=[pl.BlockSpec(memory_space=pltpu.SMEM)] + [vmem] * (1 + N_CHIP + len(extra)),
        out_specs=[vmem] * N_X,
        out_shape=[jax.ShapeDtypeStruct((2 * capacity, N_CHIP * piece), jnp.bfloat16)] * N_X,
        name="pick",
    )(shard, place, *pieces, *extra)


def split_dot(parts, weights):
    n = len(parts)
    features, width = sum(w.shape[0] for w in weights), weights[0].shape[1]
    rows = sum(p.shape[0] for p in parts)

    def kernel(*refs):
        ins, mine, theirs = refs[: n + len(weights)], refs[-2], refs[-1]
        left = jnp.concatenate([ref[...] for ref in ins[:n]], axis=0)
        right = jnp.concatenate([ref[...] for ref in ins[n:]], axis=0) if len(weights) > 1 else ins[n][...]
        total = dot(left, right, ((1,), (0,)))
        mine[...] = total[:, : width // 2]
        theirs[...] = total[:, width // 2 :]

    assert parts[0].shape[1] == features
    shape = jax.ShapeDtypeStruct((rows, width // 2), jnp.float32)
    return pl.pallas_call(kernel, out_shape=[shape] * 2, name="split_dot")(*parts, *weights)


def row_parts_of(own, other, weight, n):
    rows = own.shape[0] // n

    def kernel(own_ref, other_ref, weight_ref, *outs):
        left = jnp.concatenate([own_ref[...], other_ref[...]], axis=1)
        total = dot(left, weight_ref[...], ((1,), (1,)))
        for d, out in enumerate(outs):
            out[...] = total[d * rows : (d + 1) * rows].astype(out.dtype)

    shape = jax.ShapeDtypeStruct((rows, weight.shape[0]), jnp.bfloat16)
    return pl.pallas_call(kernel, out_shape=[shape] * n, name="row_parts")(own, other, weight)


def parts_of(own, other, pieces):
    def kernel(own_ref, other_ref, *refs):
        left = jnp.concatenate([own_ref[...], other_ref[...]], axis=1)
        for ref, out in zip(refs[: len(pieces)], refs[len(pieces) :], strict=True):
            out[...] = dot(left, ref[...], ((1,), (1,))).astype(out.dtype)

    shape = jax.ShapeDtypeStruct((own.shape[0], pieces[0].shape[0]), jnp.bfloat16)
    return pl.pallas_call(kernel, out_shape=[shape] * len(pieces), name="parts")(own, other, *pieces)


def combine(parts, place, mix):
    capacity, features = parts[0].shape[0] // 2, parts[0].shape[1]
    tokens = mix.shape[1]
    piece = features // N_CHIP

    def kernel(place_ref, mix_ref, *refs):
        ins, out = refs[:-1], refs[-1]
        number = lax.broadcasted_iota(jnp.int32, (N_X * capacity, tokens), 0)
        for block in range(2):
            rows = jnp.concatenate([ref[block * capacity : (block + 1) * capacity] for ref in ins], axis=0)
            total = jnp.zeros((tokens, features), jnp.float32)
            for n in range(2):
                chosen = jnp.where(number == place_ref[block, n : n + 1], 1.0, 0.0).astype(jnp.bfloat16)
                total = total + mix_ref[block, :, n : n + 1] * dot(chosen, rows, ((0,), (0,)))
            total = total.astype(out.dtype)
            for chip in range(N_CHIP):
                out[chip, block] = total[:, chip * piece : (chip + 1) * piece]

    shape = jax.ShapeDtypeStruct((N_CHIP, 2, tokens, piece), jnp.bfloat16)
    return pl.pallas_call(kernel, out_shape=shape, name="combine")(place, mix, *parts)


def finish(own, crossed, place):
    rows, width = own.shape

    def kernel(place_ref, own_ref, crossed_ref, out):
        tokens = out.shape[0]
        number = lax.broadcasted_iota(jnp.int32, (rows, tokens), 0)
        total = jnp.zeros(out.shape, jnp.float32)
        for b, ref in enumerate((own_ref, crossed_ref)):
            here = [number + b * rows == place_ref[n : n + 1] for n in range(2)]
            total = total + dot(jnp.where(here[0] | here[1], 1.0, 0.0).astype(jnp.bfloat16), ref[...], ((0,), (0,)))
        out[...] = total.astype(out.dtype)

    shape = jax.ShapeDtypeStruct((place.shape[1], width), jnp.bfloat16)
    return pl.pallas_call(kernel, out_shape=shape, name="finish")(place, own, crossed)


def slots_of(routes):
    flat = routes.reshape(-1)
    one_hot = (flat[:, None] == jnp.arange(2 * N_X, dtype=jnp.int32)[None, :]).astype(jnp.int32)
    earlier = jnp.cumsum(one_hot, axis=0) - one_hot
    return jnp.sum(earlier * one_hot, axis=1).reshape(routes.shape)


def feature_sum(own, other, pieces, capacity):
    half = N_CHIP // 2
    parts = parts_of(own, other, pieces[1 : half + 1]) + parts_of(own, other, pieces[half + 1 :] + pieces[:1])
    total = parts[-1].astype(jnp.float32)
    for k in range(1, N_CHIP):
        total = total + chip_swap(parts[k - 1], k).astype(jnp.float32)
    return send_home(total.astype(jnp.bfloat16), capacity)


def send_home(rows, capacity):
    width = rows.shape[1]
    shaped = rows.reshape(N_X, 2, capacity, width)
    back = [shaped[0]] + [swap(shaped[d], "x", N_X, d) for d in range(1, N_X)]
    back = jnp.stack(back, axis=1)
    crossed = swap(back[1], "z_lo", 2, 1)
    return back[0].reshape(-1, width), crossed.reshape(-1, width)


def local(tokens, routes, mix_weights, cotangent, w_gate, w_up, w_down):
    tok_dev, _ = tokens.shape
    capacity = min(tok_dev, 6 * tok_dev // (2 * N_X))
    z_lo, x = lax.axis_index("z_lo"), lax.axis_index("x")
    shard = lax.axis_index(SHARD).astype(jnp.int32)[None]

    packed_gu = pack([w_gate[0], w_up[0]], shard)
    packed_down = pack_natural(w_down[0], shard)

    routes_other, mix_other = swap(routes, "z_lo", 2, 1), swap(mix_weights, "z_lo", 2, 1)
    pair = jnp.stack([tokens, cotangent])
    pair_other = swap(pair, "z_lo", 2, 1)
    both = join(tokens, cotangent, pair_other)
    gathered = [both] + [chip_swap(both, k) for k in range(1, N_CHIP)]

    gu_pieces = exchange(packed_gu)
    down = chip_exchange(packed_down)
    down = down.reshape(-1, down.shape[2])

    homes, places = [], []
    for block_routes in (routes, routes_other):
        row = jnp.bitwise_xor(block_routes % N_X, x) * capacity + slots_of(block_routes)
        homes.append((row + jnp.bitwise_xor(block_routes // N_X, z_lo) * N_X * capacity).T)
        places.append(jnp.where(homes[-1] < N_X * capacity, homes[-1], 2 * N_X * capacity))
    home, place = homes[0], jnp.stack(places)
    mix_both = jnp.stack([mix_weights, mix_other])
    mix_turned = jnp.stack([mix_weights.T, mix_other.T])

    def to_owner(parts):
        moved = [parts[0]] + [swap(parts[d], "x", N_X, d) for d in range(1, N_X)]
        return moved, [core_swap(part) for part in moved]

    row_parts = pick(gathered, 0, place, None, shard, capacity)
    grad_parts = pick(gathered, 1, place, mix_turned, shard, capacity)
    x_own, x_other = to_owner(row_parts)
    dy_own, dy_other = to_owner(grad_parts)

    width = down.shape[1] // 2

    def features_dot(parts, weights):
        mine, theirs = split_dot(parts, weights)
        theirs = core_swap(theirs)
        return mine + theirs

    pre = features_dot(x_own, gu_pieces)
    gate_pre, up_pre = pre[:, :width], pre[:, width:]
    hidden = (gate_pre * jax.nn.sigmoid(gate_pre) * up_pre).astype(jnp.bfloat16)
    hidden, gate_pre, up_pre = lax.optimization_barrier((hidden, gate_pre, up_pre))
    sigmoid_gate = jax.nn.sigmoid(gate_pre)
    active = gate_pre * sigmoid_gate
    hidden_other = core_swap(hidden)
    out_parts = row_parts_of(hidden, hidden_other, down, N_X)
    out_parts = [out_parts[0]] + [swap(out_parts[d], "x", N_X, d) for d in range(1, N_X)]
    by_chip = combine(out_parts, place, mix_both)
    by_chip = chip_exchange(by_chip)
    out_tokens = jnp.sum(by_chip.astype(jnp.float32), axis=0)
    out_crossed = swap(out_tokens[1].astype(jnp.bfloat16), "z_lo", 2, 1)
    layer_out = out_tokens[0] + out_crossed.astype(jnp.float32)

    d_hidden = features_dot(dy_own, [down])
    d_gate = d_hidden * up_pre * sigmoid_gate * (1.0 + gate_pre * (1.0 - sigmoid_gate))
    d_gu = jnp.concatenate([d_gate.astype(jnp.bfloat16), (d_hidden * active).astype(jnp.bfloat16)], axis=1)
    dx_home = feature_sum(d_gu, core_swap(d_gu), gu_pieces, capacity)

    (grad_down,) = weight_grad(dy_own, dy_other, hidden, shard, 1, True)
    grad_gate, grad_up = weight_grad(x_own, x_other, d_gu, shard, 2, False)

    grad_tokens = finish(*dx_home, home)
    return layer_out.astype(jnp.bfloat16), grad_tokens, grad_gate, grad_up, grad_down


def solution(mesh):
    parts = Mesh(mesh.devices.reshape(2, N_X, 2, 4, 2), EXPERT + SHARD)
    weight_in, weight_out = P(EXPERT, SHARD, None), P(EXPERT, None, SHARD)
    return jax.shard_map(
        local,
        mesh=parts,
        in_specs=(P(EXPERT, SHARD), P(EXPERT, None), P(EXPERT, None), P(EXPERT, SHARD), weight_in, weight_in, weight_in),
        out_specs=(P(EXPERT, SHARD), P(EXPERT, SHARD), weight_out, weight_out, weight_out),
        check_vma=False,
    )
```

profile of v0, /device:TPU:2, one launch (start us, length us, event | category | flops | bytes accessed | tf_op | source)
XLA Modules:
  0.0 366.4 jit_solution(5553919453036160845)
XLA Ops:
  1.5 2.0 collective-permute-start.2
  3.6 3.2 pack.3
  6.8 7.9 %all-to-all-start = ((bf16[8,256,768]{2,1,0:T(8,128)(2,1)}), bf16[8,256,768]{2,1,0:T(8,128)(2,1)S(1)}, u32[]{:S(2)}, u32[]{:S(2)}) async-start(bf16[8,256,768]{2,1,0:T(8,128)(2,1)} %pack.3), calls=%async_computation | async-start | bytes 6291456 | tf_op jit(solution)/shard_map/all_to_all | solution.py:86
  17.4 2.0 collective-permute-start.3
  19.4 2.7 collective-permute-start.4
  23.1 3.5 collective-permute-start.6
  26.9 38.4 %collective-permute-done.3.refs_1_ = bf16[2,2,128,256]{3,2,1,0:T(8,128)(2,1)S(1)} collective-permute-done((bf16[2,2,128,256]{3,2,1,0:T(8,128)(2,1)}, bf16[2,2,128,256]{3,2,1,0:T(8,128)(2,1)S(1)}, u32[]{:S(2)}, u32[]{:S(2)}) %collective-permute-start.3) | collective-permute-done | bytes 262176 | tf_op jit(solution)/shard_map/ppermute | solution.py:15
  66.5 3.7 %collective-permute-done.4.refs_2_ = bf16[2,2,128,256]{3,2,1,0:T(8,128)(2,1)} collective-permute-done((bf16[2,2,128,256]{3,2,1,0:T(8,128)(2,1)}, bf16[2,2,128,256]{3,2,1,0:T(8,128)(2,1)}, u32[]{:S(2)}, u32[]{:S(2)}) %collective-permute-start.4) | collective-permute-done | bytes 262176 | tf_op jit(solution)/shard_map/ppermute | solution.py:15
  70.2 5.9 %collective-permute-start.9 = (bf16[2,2,128,256]{3,2,1,0:T(8,128)(2,1)}, bf16[2,2,128,256]{3,2,1,0:T(8,128)(2,1)}, u32[]{:S(2)}, u32[]{:S(2)}) collective-permute-start(bf16[2,2,128,256]{3,2,1,0:T(8,128)(2,1)} %join.1.refs_0_), channel_id=1, source_target_pairs={{0,14},{2,12},{4,10},{6,8},{8,6},{10,4},{12,2},{14,0},{1,15},{3,13... | collective-permute-start | bytes 786440 | tf_op jit(solution)/shard_map/ppermute | solution.py:15
  76.4 4.9 %pack.2 = (bf16[256,1536]{1,0:T(8,128)(2,1)}, bf16[256,1536]{1,0:T(8,128)(2,1)}, bf16[256,1536]{1,0:T(8,128)(2,1)}, bf16[256,1536]{1,0:T(8,128)(2,1)}, bf16[256,...) custom-call(s32[1]{0:T(128)} %bitcast.10.shard_ref, ...), custom_call_target="tpu_custom_call" | custom-call | tf_op jit(solution)/shard_map/pack/pallas_call | solution.py:47
  83.4 3.5 collective-permute-start.15
  87.5 2.4 collective-permute-done.9.refs_7_
  91.8 4.1 %pick.2 = (bf16[192,2048]{1,0:T(8,128)(2,1)}, bf16[192,2048]{1,0:T(8,128)(2,1)}, bf16[192,2048]{1,0:T(8,128)(2,1)}, bf16[192,2048]{1,0:T(8,128)(2,1)}) custom-call(s32[1]{0:T(128)} %bitcast.10.shard_ref, s32[2,2,128]{2,1,0:T(2,128)} %pad_add_fusion.place_ref, bf16[2,2,128,256]{3,2,1,0:T(8,128)(2,1)} %join.1.refs_0_, bf16[2,2,128,256]{3,2,1,0:T(8,128)(2,1)} %copy-done.10, ...), custom_call_target="tpu_custom_call" | custom-call | tf_op jit(solution)/shard_map/pick/pallas_call | solution.py:163
  95.9 7.0 %collective-permute-done.13.refs_5_.refs_0_ = bf16[256,1536]{1,0:T(8,128)(2,1)} collective-permute-done((bf16[256,1536]{1,0:T(8,128)(2,1)}, bf16[256,1536]{1,0:T(8,128)(2,1)}, u32[]{:S(2)}, u32[]{:S(2)}) %collective-permute-start.13) | collective-permute-done | bytes 786464 | tf_op jit(solution)/shard_map/ppermute | solution.py:15
  102.9 16.0 %collective-permute-done.14.refs_6_.refs_1_ = bf16[256,1536]{1,0:T(8,128)(2,1)} collective-permute-done((bf16[256,1536]{1,0:T(8,128)(2,1)}, bf16[256,1536]{1,0:T(8,128)(2,1)}, u32[]{:S(2)}, u32[]{:S(2)}) %collective-permute-start.14) | collective-permute-done | bytes 786464 | tf_op jit(solution)/shard_map/ppermute | solution.py:15
  119.0 3.9 %collective-permute-start.19 = (bf16[256,1536]{1,0:T(8,128)(2,1)}, bf16[256,1536]{1,0:T(8,128)(2,1)}, u32[]{:S(2)}, u32[]{:S(2)}) collective-permute-start(bf16[256,1536]{1,0:T(8,128)(2,1)} %get-tuple-element.53), channel_id=1, source_target_pairs={{0,14},{2,12},{4,10},{6,8},{8,6},{10,4},{12,2},{14,0},{1,15},{3,13... | collective-permute-start | bytes 2359304 | tf_op jit(solution)/shard_map/ppermute | solution.py:15
  123.4 2.4 collective-permute-start.11
  125.8 30.0 %collective-permute-done.17.refs_9_.refs_0_ = bf16[256,1536]{1,0:T(8,128)(2,1)} collective-permute-done((bf16[256,1536]{1,0:T(8,128)(2,1)}, bf16[256,1536]{1,0:T(8,128)(2,1)}, u32[]{:S(2)}, u32[]{:S(2)}) %collective-permute-start.17) | collective-permute-done | bytes 786464 | tf_op jit(solution)/shard_map/ppermute | solution.py:15
  157.3 8.6 %collective-permute-done.18.refs_10_.refs_1_ = bf16[256,1536]{1,0:T(8,128)(2,1)} collective-permute-done((bf16[256,1536]{1,0:T(8,128)(2,1)}, bf16[256,1536]{1,0:T(8,128)(2,1)}, u32[]{:S(2)}, u32[]{:S(2)}) %collective-permute-start.18) | collective-permute-done | bytes 786464 | tf_op jit(solution)/shard_map/ppermute | solution.py:15
  165.9 2.9 collective-permute-done.19.refs_11_.refs_2_
  168.8 4.4 %collective-permute-done.12.refs_3_ = bf16[192,2048]{1,0:T(8,128)(2,1)} collective-permute-done((bf16[192,2048]{1,0:T(8,128)(2,1)}, bf16[192,2048]{1,0:T(8,128)(2,1)}, u32[]{:S(2)}, u32[]{:S(2)}) %collective-permute-start.12) | collective-permute-done | bytes 786464 | tf_op jit(solution)/shard_map/ppermute | solution.py:15
  173.1 10.1 %split_dot.2 = (f32[768,768]{1,0:T(8,128)}, f32[768,768]{1,0:T(8,128)}) custom-call(bf16[192,2048]{1,0:T(8,128)(2,1)} %get-tuple-element.42.refs_0_, bf16[192,2048]{1,0:T(8,128)(2,1)} %collective-permute-done.10.refs_1_, bf16[192,2048]{1,0:T(8,128)(2,1)} %collective-permute-done.11.refs_2_, bf16[192,2048]{1,0:T(8,128)(2,1)} %collective-permute-done.12.refs_3_, ...), custom_call_target="tpu_custom_call" | custom-call | tf_op jit(solution)/shard_map/split_dot/pallas_call | solution.py:187
  184.6 2.6 collective-permute-done.1
  187.7 4.2 %pick.3 = (bf16[192,2048]{1,0:T(8,128)(2,1)}, bf16[192,2048]{1,0:T(8,128)(2,1)}, bf16[192,2048]{1,0:T(8,128)(2,1)}, bf16[192,2048]{1,0:T(8,128)(2,1)}) custom-call(s32[1]{0:T(128)} %bitcast.10.shard_ref, s32[2,2,128]{2,1,0:T(2,128)} %pad_add_fusion.place_ref, bf16[2,2,128,256]{3,2,1,0:T(8,128)(2,1)} %join.1.refs_0_, bf16[2,2,128,256]{3,2,1,0:T(8,128)(2,1)} %copy-done.10, ...), custom_call_target="tpu_custom_call" | custom-call | tf_op jit(solution)/shard_map/pick/pallas_call | solution.py:163
  191.9 1.8 collective-permute-start.26
  195.4 17.1 %collective-permute-done.26.refs_1_ = bf16[192,2048]{1,0:T(8,128)(2,1)S(1)} collective-permute-done((bf16[192,2048]{1,0:T(8,128)(2,1)}, bf16[192,2048]{1,0:T(8,128)(2,1)S(1)}, u32[]{:S(2)}, u32[]{:S(2)}) %collective-permute-start.26) | collective-permute-done | bytes 786464 | tf_op jit(solution)/shard_map/ppermute | solution.py:15
  212.5 15.1 %collective-permute-done.27.refs_2_ = bf16[192,2048]{1,0:T(8,128)(2,1)S(1)} collective-permute-done((bf16[192,2048]{1,0:T(8,128)(2,1)}, bf16[192,2048]{1,0:T(8,128)(2,1)S(1)}, u32[]{:S(2)}, u32[]{:S(2)}) %collective-permute-start.27) | collective-permute-done | bytes 786464 | tf_op jit(solution)/shard_map/ppermute | solution.py:15
  230.8 6.9 %split_dot.3 = (f32[768,384]{1,0:T(8,128)}, f32[768,384]{1,0:T(8,128)}) custom-call(bf16[192,2048]{1,0:T(8,128)(2,1)} %get-tuple-element.61.refs_0_, bf16[192,2048]{1,0:T(8,128)(2,1)} %copy-done.5, bf16[192,2048]{1,0:T(8,128)(2,1)} %copy-done.7, bf16[192,2048]{1,0:T(8,128)(2,1)} %collective-permute-done.28.refs_3_, bf16[2048,768]{1,0:T(8,128)(2,1)} %bitcast.61), custom_call_target="tpu_custom_call" | custom-call | tf_op jit(solution)/shard_map/split_dot/pallas_call | solution.py:187
  237.7 2.7 add.77
  243.1 3.2 collective-permute-done.21.other_ref
  247.2 6.4 %row_parts.1 = (bf16[192,2048]{1,0:T(8,128)(2,1)}, bf16[192,2048]{1,0:T(8,128)(2,1)}, bf16[192,2048]{1,0:T(8,128)(2,1)}, bf16[192,2048]{1,0:T(8,128)(2,1)}) custom-call(bf16[768,384]{1,0:T(8,128)(2,1)} %copy-done.2, bf16[768,384]{1,0:T(8,128)(2,1)} %copy-done.12, bf16[2048,768]{1,0:T(8,128)(2,1)} %bitcast.62), custom_call_target="tpu_custom_call" | custom-call | tf_op jit(solution)/shard_map/row_parts/pallas_call | solution.py:200
  253.6 2.9 collective-permute-start.22
  259.6 6.1 %parts.2 = (bf16[768,256]{1,0:T(8,128)(2,1)}, bf16[768,256]{1,0:T(8,128)(2,1)}, bf16[768,256]{1,0:T(8,128)(2,1)}, bf16[768,256]{1,0:T(8,128)(2,1)}) custom-call(bf16[768,768]{1,0:T(8,128)(2,1)} %copy-done.1, bf16[768,768]{1,0:T(8,128)(2,1)} %copy-done.3, bf16[256,1536]{1,0:T(8,128)(2,1)} %collective-permute-done.17.refs_9_.refs_0_, ...), custom_call_target="tpu_custom_call" | custom-call | tf_op jit(solution)/shard_map/parts/pallas_call | solution.py:210
  265.7 9.3 %collective-permute-done.22.refs_1_ = bf16[192,2048]{1,0:T(8,128)(2,1)S(1)} collective-permute-done((bf16[192,2048]{1,0:T(8,128)(2,1)}, bf16[192,2048]{1,0:T(8,128)(2,1)S(1)}, u32[]{:S(2)}, u32[]{:S(2)}) %collective-permute-start.22) | collective-permute-done | bytes 786464 | tf_op jit(solution)/shard_map/ppermute | solution.py:15
  275.4 6.5 %parts.3 = (bf16[768,256]{1,0:T(8,128)(2,1)}, bf16[768,256]{1,0:T(8,128)(2,1)}, bf16[768,256]{1,0:T(8,128)(2,1)}, bf16[768,256]{1,0:T(8,128)(2,1)}) custom-call(bf16[768,768]{1,0:T(8,128)(2,1)} %copy-done.1, bf16[768,768]{1,0:T(8,128)(2,1)} %copy-done.3, bf16[256,1536]{1,0:T(8,128)(2,1)} %collective-permute-done.13.refs_5_.refs_0_, ...), custom_call_target="tpu_custom_call" | custom-call | tf_op jit(solution)/shard_map/parts/pallas_call | solution.py:210
  281.9 11.5 %collective-permute-done.23.refs_2_ = bf16[192,2048]{1,0:T(8,128)(2,1)} collective-permute-done((bf16[192,2048]{1,0:T(8,128)(2,1)}, bf16[192,2048]{1,0:T(8,128)(2,1)}, u32[]{:S(2)}, u32[]{:S(2)}) %collective-permute-start.23) | collective-permute-done | bytes 786464 | tf_op jit(solution)/shard_map/ppermute | solution.py:15
  294.9 4.0 %collective-permute-start.31 = (bf16[768,256]{1,0:T(8,128)(2,1)}, bf16[768,256]{1,0:T(8,128)(2,1)}, u32[]{:S(2)}, u32[]{:S(2)}) collective-permute-start(bf16[768,256]{1,0:T(8,128)(2,1)} %get-tuple-element.70), channel_id=1, source_target_pairs={{0,2},{2,0},{4,6},{6,4},{8,10},{10,8},{12,14},{14,12},{1,3},{3,1},... | collective-permute-start | bytes 1179656 | tf_op jit(solution)/shard_map/ppermute | solution.py:15
  298.9 6.9 %collective-permute-done.34 = bf16[768,256]{1,0:T(8,128)(2,1)S(1)} collective-permute-done((bf16[768,256]{1,0:T(8,128)(2,1)}, bf16[768,256]{1,0:T(8,128)(2,1)S(1)}, u32[]{:S(2)}, u32[]{:S(2)}) %collective-permute-start.34) | collective-permute-done | bytes 393248 | tf_op jit(solution)/shard_map/ppermute | solution.py:15
  305.9 9.1 %collective-permute-done.33 = bf16[768,256]{1,0:T(8,128)(2,1)S(1)} collective-permute-done((bf16[768,256]{1,0:T(8,128)(2,1)}, bf16[768,256]{1,0:T(8,128)(2,1)S(1)}, u32[]{:S(2)}, u32[]{:S(2)}) %collective-permute-start.33) | collective-permute-done | bytes 393248 | tf_op jit(solution)/shard_map/ppermute | solution.py:15
  316.2 4.2 %combine.1 = bf16[8,2,128,256]{3,2,1,0:T(8,128)(2,1)} custom-call(s32[2,2,128]{2,1,0:T(2,128)} %pad_add_fusion.place_ref, f32[2,128,2]{2,1,0:T(8,128)} %copy.20.mix_ref, bf16[192,2048]{1,0:T(8,128)(2,1)} %get-tuple-element.57.refs_0_, bf16[192,2048]{1,0:T(8,128)(2,1)} %copy-done.11, bf16[192,2048]{1,0:T(8,128)(2,1)} %collective-permute-done.23.refs_2_, ...), custom_call_target="tpu_custom_call" | custom-call | tf_op jit(solution)/shard_map/combine/pallas_call | solution.py:232
  320.5 3.6 all-to-all-start.1
  324.1 2.2 add_convert_fusion
  327.5 4.8 %collective-permute-start.39 = (bf16[2,96,256]{2,1,0:T(8,128)(2,1)S(1)}, bf16[2,96,256]{2,1,0:T(8,128)(2,1)S(1)}, u32[]{:S(2)}, u32[]{:S(2)}) collective-permute-start(bf16[2,96,256]{2,1,0:T(8,128)(2,1)S(1)} %bitcast.72), channel_id=1, source_target_pairs={{0,32},{16,48},{32,0},{48,16},{1,33},{17,49},{33,1},{49,17},{2,34}... | collective-permute-start | bytes 294920 | tf_op jit(solution)/shard_map/ppermute | solution.py:15
  333.3 1.7 collective-permute-done.39
  335.0 3.4 collective-permute-start.38
  338.4 9.5 %weight_grad.3 = bf16[1,4096,384]{2,1,0:T(8,128)(2,1)} custom-call(s32[1]{0:T(128)} %bitcast.10.shard_ref, bf16[192,2048]{1,0:T(8,128)(2,1)} %get-tuple-element.61.refs_0_, bf16[192,2048]{1,0:T(8,128)(2,1)} %copy-done.5, bf16[192,2048]{1,0:T(8,128)(2,1)} %copy-done.7, bf16[192,2048]{1,0:T(8,128)(2,1)} %collective-permute-done.28.refs_3_, ...), custom_call_target="tpu_custom_call" | custom-call | flops 2415919104 | bytes 10027008 | tf_op jit(solution)/shard_map/weight_grad/pallas_call | solution.py:110
  351.9 11.3 %weight_grad.2 = (bf16[1,4096,384]{2,1,0:T(8,128)(2,1)}, bf16[1,4096,384]{2,1,0:T(8,128)(2,1)}) custom-call(s32[1]{0:T(128)} %bitcast.10.shard_ref, bf16[192,2048]{1,0:T(8,128)(2,1)} %get-tuple-element.42.refs_0_, bf16[192,2048]{1,0:T(8,128)(2,1)} %collective-permute-done.10.refs_1_, bf16[192,2048]{1,0:T(8,128)(2,1)} %collective-permute-done.11.refs_2_, ...), custom_call_target="tpu_custom_call" | custom-call | flops 4831838208 | bytes 13762560 | tf_op jit(solution)/shard_map/weight_grad/pallas_call | solution.py:110
  363.9 1.9 finish.1
  (152 shorter events, 37.0 us)
Async XLA Ops:
  1.5 13.5 %collective-permute-start.2 = (bf16[2,128,256]{2,1,0:T(8,128)(2,1)S(1)}, bf16[2,128,256]{2,1,0:T(8,128)(2,1)S(1)}, u32[]{:S(2)}, u32[]{:S(2)}) collective-permute-start(bf16[2,128,256]{2,1,0:T(8,128)(2,1)S(1)} %pad_maximum_fusion.2), channel_id=1, source_target_pairs={{0,64},{64,0},{1,65},{65,1},{2,66},{66,2},{3,67},{67,3},{4,68},{68... | collective-permute-start | bytes 393224 | tf_op jit(solution)/shard_map/ppermute | solution.py:15
  3.5 23.1 %collective-permute-start = (s32[128,2]{0,1:T(2,128)}, s32[128,2]{0,1:T(2,128)S(1)}, u32[]{:S(2)}, u32[]{:S(2)}) collective-permute-start(s32[128,2]{0,1:T(2,128)} %param.8), channel_id=1, source_target_pairs={{0,64},{64,0},{1,65},{65,1},{2,66},{66,2},{3,67},{67,3},{4,68},{68... | collective-permute-start | bytes 3080 | tf_op jit(solution)/shard_map/ppermute | solution.py:15
  6.8 222.3 %all-to-all-start = ((bf16[8,256,768]{2,1,0:T(8,128)(2,1)}), bf16[8,256,768]{2,1,0:T(8,128)(2,1)S(1)}, u32[]{:S(2)}, u32[]{:S(2)}) async-start(bf16[8,256,768]{2,1,0:T(8,128)(2,1)} %pack.3), calls=%async_computation | async-start | bytes 6291456 | tf_op jit(solution)/shard_map/all_to_all | solution.py:86
  17.4 47.9 %collective-permute-start.3 = (bf16[2,2,128,256]{3,2,1,0:T(8,128)(2,1)}, bf16[2,2,128,256]{3,2,1,0:T(8,128)(2,1)S(1)}, u32[]{:S(2)}, u32[]{:S(2)}) collective-permute-start(bf16[2,2,128,256]{3,2,1,0:T(8,128)(2,1)} %join.1.refs_0_), channel_id=1, source_target_pairs={{0,2},{2,0},{4,6},{6,4},{8,10},{10,8},{12,14},{14,12},{1,3},{3,1},... | collective-permute-start | bytes 786440 | tf_op jit(solution)/shard_map/ppermute | solution.py:15
  19.4 50.8 %collective-permute-start.4 = (bf16[2,2,128,256]{3,2,1,0:T(8,128)(2,1)}, bf16[2,2,128,256]{3,2,1,0:T(8,128)(2,1)}, u32[]{:S(2)}, u32[]{:S(2)}) collective-permute-start(bf16[2,2,128,256]{3,2,1,0:T(8,128)(2,1)} %join.1.refs_0_), channel_id=1, source_target_pairs={{0,4},{2,6},{4,0},{6,2},{8,12},{10,14},{12,8},{14,10},{1,5},{3,7},... | collective-permute-start | bytes 786440 | tf_op jit(solution)/shard_map/ppermute | solution.py:15
  23.0 59.1 %collective-permute-start.5 = (bf16[2,2,128,256]{3,2,1,0:T(8,128)(2,1)}, bf16[2,2,128,256]{3,2,1,0:T(8,128)(2,1)}, u32[]{:S(2)}, u32[]{:S(2)}) collective-permute-start(bf16[2,2,128,256]{3,2,1,0:T(8,128)(2,1)} %join.1.refs_0_), channel_id=1, source_target_pairs={{0,6},{2,4},{4,2},{6,0},{8,14},{10,12},{12,10},{14,8},{1,7},{3,5},... | collective-permute-start | bytes 786440 | tf_op jit(solution)/shard_map/ppermute | solution.py:15
  23.1 59.1 %collective-permute-start.6 = (bf16[2,2,128,256]{3,2,1,0:T(8,128)(2,1)}, bf16[2,2,128,256]{3,2,1,0:T(8,128)(2,1)}, u32[]{:S(2)}, u32[]{:S(2)}) collective-permute-start(bf16[2,2,128,256]{3,2,1,0:T(8,128)(2,1)} %join.1.refs_0_), channel_id=1, source_target_pairs={{0,8},{2,10},{4,12},{6,14},{8,0},{10,2},{12,4},{14,6},{1,9},{3,11}... | collective-permute-start | bytes 786440 | tf_op jit(solution)/shard_map/ppermute | solution.py:15
  26.6 56.7 %collective-permute-start.7 = (bf16[2,2,128,256]{3,2,1,0:T(8,128)(2,1)}, bf16[2,2,128,256]{3,2,1,0:T(8,128)(2,1)}, u32[]{:S(2)}, u32[]{:S(2)}) collective-permute-start(bf16[2,2,128,256]{3,2,1,0:T(8,128)(2,1)} %join.1.refs_0_), channel_id=1, source_target_pairs={{0,10},{2,8},{4,14},{6,12},{8,2},{10,0},{12,6},{14,4},{1,11},{3,9}... | collective-permute-start | bytes 786440 | tf_op jit(solution)/shard_map/ppermute | solution.py:15
  65.3 21.6 %collective-permute-start.8 = (bf16[2,2,128,256]{3,2,1,0:T(8,128)(2,1)}, bf16[2,2,128,256]{3,2,1,0:T(8,128)(2,1)}, u32[]{:S(2)}, u32[]{:S(2)}) collective-permute-start(bf16[2,2,128,256]{3,2,1,0:T(8,128)(2,1)} %join.1.refs_0_), channel_id=1, source_target_pairs={{0,12},{2,14},{4,8},{6,10},{8,4},{10,6},{12,0},{14,2},{1,13},{3,15... | collective-permute-start | bytes 786440 | tf_op jit(solution)/shard_map/ppermute | solution.py:15
  70.2 19.7 %collective-permute-start.9 = (bf16[2,2,128,256]{3,2,1,0:T(8,128)(2,1)}, bf16[2,2,128,256]{3,2,1,0:T(8,128)(2,1)}, u32[]{:S(2)}, u32[]{:S(2)}) collective-permute-start(bf16[2,2,128,256]{3,2,1,0:T(8,128)(2,1)} %join.1.refs_0_), channel_id=1, source_target_pairs={{0,14},{2,12},{4,10},{6,8},{8,6},{10,4},{12,2},{14,0},{1,15},{3,13... | collective-permute-start | bytes 786440 | tf_op jit(solution)/shard_map/ppermute | solution.py:15
  82.1 20.8 %collective-permute-start.13 = (bf16[256,1536]{1,0:T(8,128)(2,1)}, bf16[256,1536]{1,0:T(8,128)(2,1)}, u32[]{:S(2)}, u32[]{:S(2)}) collective-permute-start(bf16[256,1536]{1,0:T(8,128)(2,1)} %get-tuple-element.47), channel_id=1, source_target_pairs={{0,2},{2,0},{4,6},{6,4},{8,10},{10,8},{12,14},{14,12},{1,3},{3,1},... | collective-permute-start | bytes 2359304 | tf_op jit(solution)/shard_map/ppermute | solution.py:15
  82.2 36.7 %collective-permute-start.14 = (bf16[256,1536]{1,0:T(8,128)(2,1)}, bf16[256,1536]{1,0:T(8,128)(2,1)}, u32[]{:S(2)}, u32[]{:S(2)}) collective-permute-start(bf16[256,1536]{1,0:T(8,128)(2,1)} %get-tuple-element.48), channel_id=1, source_target_pairs={{0,4},{2,6},{4,0},{6,2},{8,12},{10,14},{12,8},{14,10},{1,5},{3,7},... | collective-permute-start | bytes 2359304 | tf_op jit(solution)/shard_map/ppermute | solution.py:15
  83.4 39.5 %collective-permute-start.15 = (bf16[256,1536]{1,0:T(8,128)(2,1)}, bf16[256,1536]{1,0:T(8,128)(2,1)}, u32[]{:S(2)}, u32[]{:S(2)}) collective-permute-start(bf16[256,1536]{1,0:T(8,128)(2,1)} %get-tuple-element.49), channel_id=1, source_target_pairs={{0,6},{2,4},{4,2},{6,0},{8,14},{10,12},{12,10},{14,8},{1,7},{3,5},... | collective-permute-start | bytes 2359304 | tf_op jit(solution)/shard_map/ppermute | solution.py:15
  86.9 36.5 %collective-permute-start.16 = (bf16[256,1536]{1,0:T(8,128)(2,1)}, bf16[256,1536]{1,0:T(8,128)(2,1)}, u32[]{:S(2)}, u32[]{:S(2)}) collective-permute-start(bf16[256,1536]{1,0:T(8,128)(2,1)} %get-tuple-element.50), channel_id=1, source_target_pairs={{0,8},{2,10},{4,12},{6,14},{8,0},{10,2},{12,4},{14,6},{1,9},{3,11}... | collective-permute-start | bytes 2359304 | tf_op jit(solution)/shard_map/ppermute | solution.py:15
  89.9 65.9 %collective-permute-start.17 = (bf16[256,1536]{1,0:T(8,128)(2,1)}, bf16[256,1536]{1,0:T(8,128)(2,1)}, u32[]{:S(2)}, u32[]{:S(2)}) collective-permute-start(bf16[256,1536]{1,0:T(8,128)(2,1)} %get-tuple-element.51), channel_id=1, source_target_pairs={{0,10},{2,8},{4,14},{6,12},{8,2},{10,0},{12,6},{14,4},{1,11},{3,9}... | collective-permute-start | bytes 2359304 | tf_op jit(solution)/shard_map/ppermute | solution.py:15
  102.9 62.9 %collective-permute-start.18 = (bf16[256,1536]{1,0:T(8,128)(2,1)}, bf16[256,1536]{1,0:T(8,128)(2,1)}, u32[]{:S(2)}, u32[]{:S(2)}) collective-permute-start(bf16[256,1536]{1,0:T(8,128)(2,1)} %get-tuple-element.52), channel_id=1, source_target_pairs={{0,12},{2,14},{4,8},{6,10},{8,4},{10,6},{12,0},{14,2},{1,13},{3,15... | collective-permute-start | bytes 2359304 | tf_op jit(solution)/shard_map/ppermute | solution.py:15
  119.0 49.8 %collective-permute-start.19 = (bf16[256,1536]{1,0:T(8,128)(2,1)}, bf16[256,1536]{1,0:T(8,128)(2,1)}, u32[]{:S(2)}, u32[]{:S(2)}) collective-permute-start(bf16[256,1536]{1,0:T(8,128)(2,1)} %get-tuple-element.53), channel_id=1, source_target_pairs={{0,14},{2,12},{4,10},{6,8},{8,6},{10,4},{12,2},{14,0},{1,15},{3,13... | collective-permute-start | bytes 2359304 | tf_op jit(solution)/shard_map/ppermute | solution.py:15
  122.8 45.9 %collective-permute-start.10 = (bf16[192,2048]{1,0:T(8,128)(2,1)}, bf16[192,2048]{1,0:T(8,128)(2,1)}, u32[]{:S(2)}, u32[]{:S(2)}) collective-permute-start(bf16[192,2048]{1,0:T(8,128)(2,1)} %get-tuple-element.43), channel_id=1, source_target_pairs={{0,16},{16,0},{32,48},{48,32},{1,17},{17,1},{33,49},{49,33},{2,18}... | collective-permute-start | bytes 2359304 | tf_op jit(solution)/shard_map/ppermute | solution.py:15
  123.4 45.4 %collective-permute-start.11 = (bf16[192,2048]{1,0:T(8,128)(2,1)}, bf16[192,2048]{1,0:T(8,128)(2,1)}, u32[]{:S(2)}, u32[]{:S(2)}) collective-permute-start(bf16[192,2048]{1,0:T(8,128)(2,1)} %get-tuple-element.44), channel_id=1, source_target_pairs={{0,32},{16,48},{32,0},{48,16},{1,33},{17,49},{33,1},{49,17},{2,34}... | collective-permute-start | bytes 2359304 | tf_op jit(solution)/shard_map/ppermute | solution.py:15
  155.8 17.3 %collective-permute-start.12 = (bf16[192,2048]{1,0:T(8,128)(2,1)}, bf16[192,2048]{1,0:T(8,128)(2,1)}, u32[]{:S(2)}, u32[]{:S(2)}) collective-permute-start(bf16[192,2048]{1,0:T(8,128)(2,1)} %get-tuple-element.45), channel_id=1, source_target_pairs={{0,48},{16,32},{32,16},{48,0},{1,49},{17,33},{33,17},{49,1},{2,50}... | collective-permute-start | bytes 2359304 | tf_op jit(solution)/shard_map/ppermute | solution.py:15
  183.3 54.5 %collective-permute-start.20 = (f32[768,768]{1,0:T(8,128)}, f32[768,768]{1,0:T(8,128)}, u32[]{:S(2)}, u32[]{:S(2)}) collective-permute-start(f32[768,768]{1,0:T(8,128)} %get-tuple-element.55), channel_id=1, source_target_pairs={{0,1},{1,0},{2,3},{3,2},{4,5},{5,4},{6,7},{7,6},{8,9},{9,8},{10,11... | collective-permute-start | bytes 7077896 | tf_op jit(solution)/shard_map/ppermute | solution.py:15
  191.9 20.6 %collective-permute-start.26 = (bf16[192,2048]{1,0:T(8,128)(2,1)}, bf16[192,2048]{1,0:T(8,128)(2,1)S(1)}, u32[]{:S(2)}, u32[]{:S(2)}) collective-permute-start(bf16[192,2048]{1,0:T(8,128)(2,1)} %get-tuple-element.62), channel_id=1, source_target_pairs={{0,16},{16,0},{32,48},{48,32},{1,17},{17,1},{33,49},{49,33},{2,18}... | collective-permute-start | bytes 2359304 | tf_op jit(solution)/shard_map/ppermute | solution.py:15
  193.7 33.9 %collective-permute-start.27 = (bf16[192,2048]{1,0:T(8,128)(2,1)}, bf16[192,2048]{1,0:T(8,128)(2,1)S(1)}, u32[]{:S(2)}, u32[]{:S(2)}) collective-permute-start(bf16[192,2048]{1,0:T(8,128)(2,1)} %get-tuple-element.63), channel_id=1, source_target_pairs={{0,32},{16,48},{32,0},{48,16},{1,33},{17,49},{33,1},{49,17},{2,34}... | collective-permute-start | bytes 2359304 | tf_op jit(solution)/shard_map/ppermute | solution.py:15
  193.9 35.2 %collective-permute-start.28 = (bf16[192,2048]{1,0:T(8,128)(2,1)}, bf16[192,2048]{1,0:T(8,128)(2,1)}, u32[]{:S(2)}, u32[]{:S(2)}) collective-permute-start(bf16[192,2048]{1,0:T(8,128)(2,1)} %get-tuple-element.64), channel_id=1, source_target_pairs={{0,48},{16,32},{32,16},{48,0},{1,49},{17,33},{33,17},{49,1},{2,50}... | collective-permute-start | bytes 2359304 | tf_op jit(solution)/shard_map/ppermute | solution.py:15
  242.4 16.2 %collective-permute-start.30 = (bf16[768,768]{1,0:T(8,128)(2,1)S(1)}, bf16[768,768]{1,0:T(8,128)(2,1)S(1)}, u32[]{:S(2)}, u32[]{:S(2)}) collective-permute-start(bf16[768,768]{1,0:T(8,128)(2,1)S(1)} %pad_maximum_fusion.own_ref.refs_8_), channel_id=1, source_target_pairs={{0,1},{1,0},{2,3},{3,2},{4,5},{5,4},{6,7},{7,6},{8,9},{9,8},{10,11... | collective-permute-start | bytes 3538952 | tf_op jit(solution)/shard_map/ppermute | solution.py:15
  253.6 21.5 %collective-permute-start.22 = (bf16[192,2048]{1,0:T(8,128)(2,1)}, bf16[192,2048]{1,0:T(8,128)(2,1)S(1)}, u32[]{:S(2)}, u32[]{:S(2)}) collective-permute-start(bf16[192,2048]{1,0:T(8,128)(2,1)} %get-tuple-element.58), channel_id=1, source_target_pairs={{0,16},{16,0},{32,48},{48,32},{1,17},{17,1},{33,49},{49,33},{2,18}... | collective-permute-start | bytes 2359304 | tf_op jit(solution)/shard_map/ppermute | solution.py:15
  256.4 36.9 %collective-permute-start.23 = (bf16[192,2048]{1,0:T(8,128)(2,1)}, bf16[192,2048]{1,0:T(8,128)(2,1)}, u32[]{:S(2)}, u32[]{:S(2)}) collective-permute-start(bf16[192,2048]{1,0:T(8,128)(2,1)} %get-tuple-element.59), channel_id=1, source_target_pairs={{0,32},{16,48},{32,0},{48,16},{1,33},{17,49},{33,1},{49,17},{2,34}... | collective-permute-start | bytes 2359304 | tf_op jit(solution)/shard_map/ppermute | solution.py:15
  258.1 36.7 %collective-permute-start.24 = (bf16[192,2048]{1,0:T(8,128)(2,1)}, bf16[192,2048]{1,0:T(8,128)(2,1)}, u32[]{:S(2)}, u32[]{:S(2)}) collective-permute-start(bf16[192,2048]{1,0:T(8,128)(2,1)} %get-tuple-element.60), channel_id=1, source_target_pairs={{0,48},{16,32},{32,16},{48,0},{1,49},{17,33},{33,17},{49,1},{2,50}... | collective-permute-start | bytes 2359304 | tf_op jit(solution)/shard_map/ppermute | solution.py:15
  265.7 29.1 %collective-permute-start.37 = (bf16[768,256]{1,0:T(8,128)(2,1)}, bf16[768,256]{1,0:T(8,128)(2,1)S(1)}, u32[]{:S(2)}, u32[]{:S(2)}) collective-permute-start(bf16[768,256]{1,0:T(8,128)(2,1)} %get-tuple-element.76), channel_id=1, source_target_pairs={{0,14},{2,12},{4,10},{6,8},{8,6},{10,4},{12,2},{14,0},{1,15},{3,13... | collective-permute-start | bytes 1179656 | tf_op jit(solution)/shard_map/ppermute | solution.py:15
  265.7 29.2 %collective-permute-start.36 = (bf16[768,256]{1,0:T(8,128)(2,1)}, bf16[768,256]{1,0:T(8,128)(2,1)}, u32[]{:S(2)}, u32[]{:S(2)}) collective-permute-start(bf16[768,256]{1,0:T(8,128)(2,1)} %get-tuple-element.75), channel_id=1, source_target_pairs={{0,12},{2,14},{4,8},{6,10},{8,4},{10,6},{12,0},{14,2},{1,13},{3,15... | collective-permute-start | bytes 1179656 | tf_op jit(solution)/shard_map/ppermute | solution.py:15
  275.0 23.9 %collective-permute-start.35 = (bf16[768,256]{1,0:T(8,128)(2,1)}, bf16[768,256]{1,0:T(8,128)(2,1)}, u32[]{:S(2)}, u32[]{:S(2)}) collective-permute-start(bf16[768,256]{1,0:T(8,128)(2,1)} %get-tuple-element.74), channel_id=1, source_target_pairs={{0,10},{2,8},{4,14},{6,12},{8,2},{10,0},{12,6},{14,4},{1,11},{3,9}... | collective-permute-start | bytes 1179656 | tf_op jit(solution)/shard_map/ppermute | solution.py:15
  293.4 12.5 %collective-permute-start.34 = (bf16[768,256]{1,0:T(8,128)(2,1)}, bf16[768,256]{1,0:T(8,128)(2,1)S(1)}, u32[]{:S(2)}, u32[]{:S(2)}) collective-permute-start(bf16[768,256]{1,0:T(8,128)(2,1)} %get-tuple-element.73), channel_id=1, source_target_pairs={{0,8},{2,10},{4,12},{6,14},{8,0},{10,2},{12,4},{14,6},{1,9},{3,11}... | collective-permute-start | bytes 1179656 | tf_op jit(solution)/shard_map/ppermute | solution.py:15
  294.8 20.1 %collective-permute-start.33 = (bf16[768,256]{1,0:T(8,128)(2,1)}, bf16[768,256]{1,0:T(8,128)(2,1)S(1)}, u32[]{:S(2)}, u32[]{:S(2)}) collective-permute-start(bf16[768,256]{1,0:T(8,128)(2,1)} %get-tuple-element.72), channel_id=1, source_target_pairs={{0,6},{2,4},{4,2},{6,0},{8,14},{10,12},{12,10},{14,8},{1,7},{3,5},... | collective-permute-start | bytes 1179656 | tf_op jit(solution)/shard_map/ppermute | solution.py:15
  294.8 20.1 %collective-permute-start.32 = (bf16[768,256]{1,0:T(8,128)(2,1)}, bf16[768,256]{1,0:T(8,128)(2,1)}, u32[]{:S(2)}, u32[]{:S(2)}) collective-permute-start(bf16[768,256]{1,0:T(8,128)(2,1)} %get-tuple-element.71), channel_id=1, source_target_pairs={{0,4},{2,6},{4,0},{6,2},{8,12},{10,14},{12,8},{14,10},{1,5},{3,7},... | collective-permute-start | bytes 1179656 | tf_op jit(solution)/shard_map/ppermute | solution.py:15
  294.9 29.2 %collective-permute-start.31 = (bf16[768,256]{1,0:T(8,128)(2,1)}, bf16[768,256]{1,0:T(8,128)(2,1)}, u32[]{:S(2)}, u32[]{:S(2)}) collective-permute-start(bf16[768,256]{1,0:T(8,128)(2,1)} %get-tuple-element.70), channel_id=1, source_target_pairs={{0,2},{2,0},{4,6},{6,4},{8,10},{10,8},{12,14},{14,12},{1,3},{3,1},... | collective-permute-start | bytes 1179656 | tf_op jit(solution)/shard_map/ppermute | solution.py:15
  298.9 28.5 %collective-permute-start.46 = (bf16[192,2048]{1,0:T(8,128)(2,1)S(1)}, bf16[192,2048]{1,0:T(8,128)(2,1)}, u32[]{:S(2)}, u32[]{:S(2)}) collective-permute-start(bf16[192,2048]{1,0:T(8,128)(2,1)S(1)} %copy-done.4), channel_id=1, source_target_pairs={{0,1},{1,0},{2,3},{3,2},{4,5},{5,4},{6,7},{7,6},{8,9},{9,8},{10,11... | collective-permute-start | bytes 2359304 | tf_op jit(solution)/shard_map/ppermute | solution.py:15
  305.9 26.4 %collective-permute-start.47 = (bf16[192,2048]{1,0:T(8,128)(2,1)S(1)}, bf16[192,2048]{1,0:T(8,128)(2,1)}, u32[]{:S(2)}, u32[]{:S(2)}) collective-permute-start(bf16[192,2048]{1,0:T(8,128)(2,1)S(1)} %copy-done.6), channel_id=1, source_target_pairs={{0,1},{1,0},{2,3},{3,2},{4,5},{5,4},{6,7},{7,6},{8,9},{9,8},{10,11... | collective-permute-start | bytes 2359304 | tf_op jit(solution)/shard_map/ppermute | solution.py:15
  314.9 17.3 %collective-permute-start.48 = (bf16[192,2048]{1,0:T(8,128)(2,1)S(1)}, bf16[192,2048]{1,0:T(8,128)(2,1)}, u32[]{:S(2)}, u32[]{:S(2)}) collective-permute-start(bf16[192,2048]{1,0:T(8,128)(2,1)S(1)} %copy-done.8), channel_id=1, source_target_pairs={{0,1},{1,0},{2,3},{3,2},{4,5},{5,4},{6,7},{7,6},{8,9},{9,8},{10,11... | collective-permute-start | bytes 2359304 | tf_op jit(solution)/shard_map/ppermute | solution.py:15
  314.9 17.8 %collective-permute-start.49 = (bf16[192,2048]{1,0:T(8,128)(2,1)}, bf16[192,2048]{1,0:T(8,128)(2,1)}, u32[]{:S(2)}, u32[]{:S(2)}) collective-permute-start(bf16[192,2048]{1,0:T(8,128)(2,1)} %collective-permute-done.28.refs_3_), channel_id=1, source_target_pairs={{0,1},{1,0},{2,3},{3,2},{4,5},{5,4},{6,7},{7,6},{8,9},{9,8},{10,11... | collective-permute-start | bytes 2359304 | tf_op jit(solution)/shard_map/ppermute | solution.py:15
  320.5 30.1 %all-to-all-start.1 = ((bf16[8,2,128,256]{3,2,1,0:T(8,128)(2,1)}), bf16[8,2,128,256]{3,2,1,0:T(8,128)(2,1)S(1)}, u32[]{:S(2)}, u32[]{:S(2)}) async-start(bf16[8,2,128,256]{3,2,1,0:T(8,128)(2,1)} %combine.1), calls=%async_computation.1 | async-start | bytes 2097152 | tf_op jit(solution)/shard_map/all_to_all | solution.py:86
  327.5 7.5 %collective-permute-start.39 = (bf16[2,96,256]{2,1,0:T(8,128)(2,1)S(1)}, bf16[2,96,256]{2,1,0:T(8,128)(2,1)S(1)}, u32[]{:S(2)}, u32[]{:S(2)}) collective-permute-start(bf16[2,96,256]{2,1,0:T(8,128)(2,1)S(1)} %bitcast.72), channel_id=1, source_target_pairs={{0,32},{16,48},{32,0},{48,16},{1,33},{17,49},{33,1},{49,17},{2,34}... | collective-permute-start | bytes 294920 | tf_op jit(solution)/shard_map/ppermute | solution.py:15
  332.2 18.5 %collective-permute-start.42 = (bf16[192,2048]{1,0:T(8,128)(2,1)}, bf16[192,2048]{1,0:T(8,128)(2,1)S(1)}, u32[]{:S(2)}, u32[]{:S(2)}) collective-permute-start(bf16[192,2048]{1,0:T(8,128)(2,1)} %get-tuple-element.42.refs_0_), channel_id=1, source_target_pairs={{0,1},{1,0},{2,3},{3,2},{4,5},{5,4},{6,7},{7,6},{8,9},{9,8},{10,11... | collective-permute-start | bytes 2359304 | tf_op jit(solution)/shard_map/ppermute | solution.py:15
  332.2 19.6 %collective-permute-start.43 = (bf16[192,2048]{1,0:T(8,128)(2,1)}, bf16[192,2048]{1,0:T(8,128)(2,1)}, u32[]{:S(2)}, u32[]{:S(2)}) collective-permute-start(bf16[192,2048]{1,0:T(8,128)(2,1)} %collective-permute-done.10.refs_1_), channel_id=1, source_target_pairs={{0,1},{1,0},{2,3},{3,2},{4,5},{5,4},{6,7},{7,6},{8,9},{9,8},{10,11... | collective-permute-start | bytes 2359304 | tf_op jit(solution)/shard_map/ppermute | solution.py:15
  332.8 19.1 %collective-permute-start.44 = (bf16[192,2048]{1,0:T(8,128)(2,1)}, bf16[192,2048]{1,0:T(8,128)(2,1)}, u32[]{:S(2)}, u32[]{:S(2)}) collective-permute-start(bf16[192,2048]{1,0:T(8,128)(2,1)} %collective-permute-done.11.refs_2_), channel_id=1, source_target_pairs={{0,1},{1,0},{2,3},{3,2},{4,5},{5,4},{6,7},{7,6},{8,9},{9,8},{10,11... | collective-permute-start | bytes 2359304 | tf_op jit(solution)/shard_map/ppermute | solution.py:15
  332.8 19.0 %collective-permute-start.45 = (bf16[192,2048]{1,0:T(8,128)(2,1)}, bf16[192,2048]{1,0:T(8,128)(2,1)}, u32[]{:S(2)}, u32[]{:S(2)}) collective-permute-start(bf16[192,2048]{1,0:T(8,128)(2,1)} %collective-permute-done.12.refs_3_), channel_id=1, source_target_pairs={{0,1},{1,0},{2,3},{3,2},{4,5},{5,4},{6,7},{7,6},{8,9},{9,8},{10,11... | collective-permute-start | bytes 2359304 | tf_op jit(solution)/shard_map/ppermute | solution.py:15
  335.0 12.9 %collective-permute-start.38 = (bf16[2,96,256]{2,1,0:T(8,128)(2,1)}, bf16[2,96,256]{2,1,0:T(8,128)(2,1)S(1)}, u32[]{:S(2)}, u32[]{:S(2)}) collective-permute-start(bf16[2,96,256]{2,1,0:T(8,128)(2,1)} %bitcast.25), channel_id=1, source_target_pairs={{0,16},{16,0},{32,48},{48,32},{1,17},{17,1},{33,49},{49,33},{2,18}... | collective-permute-start | bytes 294920 | tf_op jit(solution)/shard_map/ppermute | solution.py:15
  349.6 13.6 %collective-permute-start.41 = (bf16[4,96,256]{2,1,0:T(8,128)(2,1)S(1)}, bf16[4,96,256]{2,1,0:T(8,128)(2,1)S(1)}, u32[]{:S(2)}, u32[]{:S(2)}) collective-permute-start(bf16[4,96,256]{2,1,0:T(8,128)(2,1)S(1)} %get-tuple-element.86), channel_id=1, source_target_pairs={{0,64},{64,0},{1,65},{65,1},{2,66},{66,2},{3,67},{67,3},{4,68},{68... | collective-permute-start | bytes 589832 | tf_op jit(solution)/shard_map/ppermute | solution.py:15
  350.8 15.0 %collective-permute-start.25 = (bf16[128,256]{1,0:T(8,128)(2,1)S(1)}, bf16[128,256]{1,0:T(8,128)(2,1)S(1)}, u32[]{:S(2)}, u32[]{:S(2)}) collective-permute-start(bf16[128,256]{1,0:T(8,128)(2,1)S(1)} %fusion.2), channel_id=1, source_target_pairs={{0,64},{64,0},{1,65},{65,1},{2,66},{66,2},{3,67},{67,3},{4,68},{68... | collective-permute-start | bytes 196616 | tf_op jit(solution)/shard_map/ppermute | solution.py:15
  (25 other events, 233.9 us)
where the time goes:
time: 368 us; the launch traced here: 366 us
  waiting for transfers between devices  192 us (52%)
  Pallas kernels  81.1 us (22%)
  starting transfers between devices  70.1 us (19%)
  other arithmetic  11.9 us (3%)
  local copies, waits for them, and re-layouts  10.4 us (3%)
    ppermute x50, waiting for transfers between devices, swap(): return lax.ppermute(value, axes, [(i, i ^ offset) for i in range(size)])  192 us
    ppermute x50, starting transfers between devices, swap(): return lax.ppermute(value, axes, [(i, i ^ offset) for i in range(size)])  58.5 us
    pallas_call x2, Pallas kernels, weight_grad(): pl.pallas_call(kernel, grid_spec=pltpu.PrefetchScalarGridSpec(num_scalar_...  20.8 us
    pallas_call x2, Pallas kernels, split_dot(): pl.pallas_call(kernel, out_shape=[shape] * 2, name='split_dot')  17 us
    pallas_call x2, Pallas kernels, parts_of(): pl.pallas_call(kernel, out_shape=[shape] * len(pieces), name='parts')  12.6 us
    all_to_all x2, starting transfers between devices, chip_exchange(): lax.all_to_all(value, ('z_hi', 'y'), split_axis=0, concat_axis=0, tiled=T...  11.5 us
    pallas_call x2, Pallas kernels, pick(): pl.pallas_call(kernel, in_specs=[pl.BlockSpec(memory_space=pltpu.SMEM)] +...  8.32 us
  transfers between devices with their start and end apart: 52, of which 20 were waited for; matrix products, arithmetic and copies ran while one was open for 4% of the time, Pallas kernels for 22%

commit v1 on v0

--- a/solution.py
+++ b/solution.py
@@ -96,22 +96,28 @@
     width = right.shape[1] // n_out
 
     def kernel(shard_ref, *refs):
-        core = shard_ref[0] % 2
+        chip, core = shard_ref[0] // 2, shard_ref[0] % 2
         right_ref, outs = refs[2 * N_X], refs[2 * N_X + 1 :]
-        for ins, place in ((refs[:N_X], core), (refs[N_X : 2 * N_X], 1 - core)):
-            left = jnp.concatenate([ref[...] for ref in ins], axis=0)
-            total = dot(left, right_ref[...], ((0,), (0,))).astype(outs[0].dtype)
-            at = pl.ds(pl.multiple_of(place * piece, piece), piece)
-            for n, out in enumerate(outs):
-                out[0, at, :] = total[:, n * width : (n + 1) * width]
-
-    in_block = pl.BlockSpec((rows, piece), lambda k, s: (0, k))
-    out_block = pl.BlockSpec((1, 2 * piece, width), lambda k, s: (0, k if natural else jnp.bitwise_xor(s[0] // 2, k), 0))
+        sides = [jnp.concatenate([ref[...] for ref in refs[i * N_X : (i + 1) * N_X]], axis=0) for i in range(2)]
+        total = dot(jnp.concatenate(sides, axis=1), right_ref[...], ((0,), (0,))).astype(outs[0].dtype)
+        for side, place in enumerate((core, 1 - core)):
+            for j in range(2):
+                to = 2 * (j if natural else jnp.bitwise_xor(j, chip % 2)) + place
+                at = pl.ds(pl.multiple_of(to * piece, piece), piece)
+                start = (2 * side + j) * piece
+                for n, out in enumerate(outs):
+                    out[0, at, :] = total[start : start + piece, n * width : (n + 1) * width]
+
+    def out_index(k, s):
+        return 0, k if natural else jnp.bitwise_xor(s[0] // 4, k), 0
+
+    in_block = pl.BlockSpec((rows, 2 * piece), lambda k, s: (0, k))
+    out_block = pl.BlockSpec((1, 4 * piece, width), out_index)
     return pl.pallas_call(
         kernel,
         grid_spec=pltpu.PrefetchScalarGridSpec(
             num_scalar_prefetch=1,
-            grid=(N_CHIP,),
+            grid=(N_CHIP // 2,),
             in_specs=[in_block] * (2 * N_X) + [pl.BlockSpec(right.shape, lambda k, s: (0, 0))],
             out_specs=[out_block] * n_out,
         ),
@@ -212,18 +218,21 @@
 
 def combine(parts, place, mix):
     capacity, features = parts[0].shape[0] // 2, parts[0].shape[1]
-    tokens = mix.shape[1]
+    tokens = mix.shape[2]
     piece = features // N_CHIP
 
     def kernel(place_ref, mix_ref, *refs):
         ins, out = refs[:-1], refs[-1]
         number = lax.broadcasted_iota(jnp.int32, (N_X * capacity, tokens), 0)
+        square = (tokens, tokens)
+        same = lax.broadcasted_iota(jnp.int32, square, 0) == lax.broadcasted_iota(jnp.int32, square, 1)
         for block in range(2):
             rows = jnp.concatenate([ref[block * capacity : (block + 1) * capacity] for ref in ins], axis=0)
             total = jnp.zeros((tokens, features), jnp.float32)
             for n in range(2):
                 chosen = jnp.where(number == place_ref[block, n : n + 1], 1.0, 0.0).astype(jnp.bfloat16)
-                total = total + mix_ref[block, :, n : n + 1] * dot(chosen, rows, ((0,), (0,)))
+                share = jnp.sum(jnp.where(same, mix_ref[block, n : n + 1], 0.0), axis=1, keepdims=True)
+                total = total + share * dot(chosen, rows, ((0,), (0,)))
             total = total.astype(out.dtype)
             for chip in range(N_CHIP):
                 out[chip, block] = total[:, chip * piece : (chip + 1) * piece]
@@ -257,10 +266,11 @@
 
 def feature_sum(own, other, pieces, capacity):
     half = N_CHIP // 2
-    parts = parts_of(own, other, pieces[1 : half + 1]) + parts_of(own, other, pieces[half + 1 :] + pieces[:1])
-    total = parts[-1].astype(jnp.float32)
+    far = parts_of(own, other, pieces[half : half + 2]) + parts_of(own, other, pieces[half + 2 :])
+    near = parts_of(own, other, pieces[:half])
+    total = near[0].astype(jnp.float32)
     for k in range(1, N_CHIP):
-        total = total + chip_swap(parts[k - 1], k).astype(jnp.float32)
+        total = total + chip_swap((near + far)[k], k).astype(jnp.float32)
     return send_home(total.astype(jnp.bfloat16), capacity)
 
 
@@ -298,11 +308,12 @@
         homes.append((row + jnp.bitwise_xor(block_routes // N_X, z_lo) * N_X * capacity).T)
         places.append(jnp.where(homes[-1] < N_X * capacity, homes[-1], 2 * N_X * capacity))
     home, place = homes[0], jnp.stack(places)
-    mix_both = jnp.stack([mix_weights, mix_other])
     mix_turned = jnp.stack([mix_weights.T, mix_other.T])
 
     def to_owner(parts):
-        moved = [parts[0]] + [swap(parts[d], "x", N_X, d) for d in range(1, N_X)]
+        moved = [parts[0]]
+        for d in range(1, N_X):
+            moved.append(swap(parts[d], "x", N_X, d))
         return moved, [core_swap(part) for part in moved]
 
     row_parts = pick(gathered, 0, place, None, shard, capacity)
@@ -326,7 +337,7 @@
     hidden_other = core_swap(hidden)
     out_parts = row_parts_of(hidden, hidden_other, down, N_X)
     out_parts = [out_parts[0]] + [swap(out_parts[d], "x", N_X, d) for d in range(1, N_X)]
-    by_chip = combine(out_parts, place, mix_both)
+    by_chip = combine(out_parts, place, mix_turned)
     by_chip = chip_exchange(by_chip)
     out_tokens = jnp.sum(by_chip.astype(jnp.float32), axis=0)
     out_crossed = swap(out_tokens[1].astype(jnp.bfloat16), "z_lo", 2, 1)

time: 368 us -> 364 us (0.989)
    unnamed x43 -> x47, local copies, waits for them, and re-layouts: 6.71 us -> 9.16 us
    pallas_call x2 -> x3, Pallas kernels: 12.6 us -> 15 us  [parts_of(): pl.pallas_call(kernel, out_shape=[shape] * len(pieces), name='parts')]
  transfers between devices with their start and end apart: 52 -> 52, of which waited for: 20 -> 20; matrix products, arithmetic and copies ran while one was open for 4% -> 3% of each run, Pallas kernels for 22% -> 22%
where the time goes in v1:
time: 364 us; the launch traced here: 363 us
  waiting for transfers between devices  189 us (52%)
  Pallas kernels  79.7 us (22%)
  starting transfers between devices  69.1 us (19%)
  local copies, waits for them, and re-layouts  12 us (3%)
  other arithmetic  11.9 us (3%)
    ppermute x50, waiting for transfers between devices, swap(): return lax.ppermute(value, axes, [(i, i ^ offset) for i in range(size)])  189 us
    ppermute x50, starting transfers between devices, swap(): return lax.ppermute(value, axes, [(i, i ^ offset) for i in range(size)])  57.6 us
    pallas_call x2, Pallas kernels, weight_grad(): pl.pallas_call(kernel, grid_spec=pltpu.PrefetchScalarGridSpec(num_scalar_...  17.3 us
    pallas_call x2, Pallas kernels, split_dot(): pl.pallas_call(kernel, out_shape=[shape] * 2, name='split_dot')  17 us
    pallas_call x3, Pallas kernels, parts_of(): pl.pallas_call(kernel, out_shape=[shape] * len(pieces), name='parts')  15 us
    all_to_all x2, starting transfers between devices, chip_exchange(): lax.all_to_all(value, ('z_hi', 'y'), split_axis=0, concat_axis=0, tiled=T...  11.5 us
    unnamed x47, local copies, waits for them, and re-layouts  9.16 us
    pallas_call x2, Pallas kernels, pick(): pl.pallas_call(kernel, in_specs=[pl.BlockSpec(memory_space=pltpu.SMEM)] +...  8.2 us
  transfers between devices with their start and end apart: 52, of which 20 were waited for; matrix products, arithmetic and copies ran while one was open for 3% of the time, Pallas kernels for 22%

profile of v1, /device:TPU:2, one launch (start us, length us, event | category | flops | bytes accessed | tf_op | source)
XLA Modules:
  0.0 362.6 jit_solution(4644668998876304275)
XLA Ops:
  1.5 2.0 collective-permute-start.2
  3.6 3.2 pack.3
  6.8 7.9 %all-to-all-start = ((bf16[8,256,768]{2,1,0:T(8,128)(2,1)}), bf16[8,256,768]{2,1,0:T(8,128)(2,1)S(1)}, u32[]{:S(2)}, u32[]{:S(2)}) async-start(bf16[8,256,768]{2,1,0:T(8,128)(2,1)} %pack.3), calls=%async_computation | async-start | bytes 6291456 | tf_op jit(solution)/shard_map/all_to_all | solution.py:86
  17.4 2.0 collective-permute-start.3
  19.4 2.7 collective-permute-start.4
  23.1 3.5 collective-permute-start.6
  26.9 38.4 %collective-permute-done.3.refs_1_ = bf16[2,2,128,256]{3,2,1,0:T(8,128)(2,1)S(1)} collective-permute-done((bf16[2,2,128,256]{3,2,1,0:T(8,128)(2,1)}, bf16[2,2,128,256]{3,2,1,0:T(8,128)(2,1)S(1)}, u32[]{:S(2)}, u32[]{:S(2)}) %collective-permute-start.3) | collective-permute-done | bytes 262176 | tf_op jit(solution)/shard_map/ppermute | solution.py:15
  66.5 3.7 %collective-permute-done.4.refs_2_ = bf16[2,2,128,256]{3,2,1,0:T(8,128)(2,1)} collective-permute-done((bf16[2,2,128,256]{3,2,1,0:T(8,128)(2,1)}, bf16[2,2,128,256]{3,2,1,0:T(8,128)(2,1)}, u32[]{:S(2)}, u32[]{:S(2)}) %collective-permute-start.4) | collective-permute-done | bytes 262176 | tf_op jit(solution)/shard_map/ppermute | solution.py:15
  70.2 5.9 %collective-permute-start.9 = (bf16[2,2,128,256]{3,2,1,0:T(8,128)(2,1)}, bf16[2,2,128,256]{3,2,1,0:T(8,128)(2,1)}, u32[]{:S(2)}, u32[]{:S(2)}) collective-permute-start(bf16[2,2,128,256]{3,2,1,0:T(8,128)(2,1)} %join.1.refs_0_), channel_id=1, source_target_pairs={{0,14},{2,12},{4,10},{6,8},{8,6},{10,4},{12,2},{14,0},{1,15},{3,13... | collective-permute-start | bytes 786440 | tf_op jit(solution)/shard_map/ppermute | solution.py:15
  76.4 4.9 %pack.2 = (bf16[256,1536]{1,0:T(8,128)(2,1)}, bf16[256,1536]{1,0:T(8,128)(2,1)}, bf16[256,1536]{1,0:T(8,128)(2,1)}, bf16[256,1536]{1,0:T(8,128)(2,1)}, bf16[256,...) custom-call(s32[1]{0:T(128)} %bitcast.12.shard_ref, ...), custom_call_target="tpu_custom_call" | custom-call | tf_op jit(solution)/shard_map/pack/pallas_call | solution.py:47
  83.4 3.5 collective-permute-start.15
  87.4 2.5 collective-permute-done.9.refs_7_
  91.8 4.1 %pick.2 = (bf16[192,2048]{1,0:T(8,128)(2,1)}, bf16[192,2048]{1,0:T(8,128)(2,1)}, bf16[192,2048]{1,0:T(8,128)(2,1)}, bf16[192,2048]{1,0:T(8,128)(2,1)}) custom-call(s32[1]{0:T(128)} %bitcast.12.shard_ref, s32[2,2,128]{2,1,0:T(2,128)} %pad_add_fusion.place_ref, bf16[2,2,128,256]{3,2,1,0:T(8,128)(2,1)} %join.1.refs_0_, bf16[2,2,128,256]{3,2,1,0:T(8,128)(2,1)} %copy-done.10, ...), custom_call_target="tpu_custom_call" | custom-call | tf_op jit(solution)/shard_map/pick/pallas_call | solution.py:169
  95.9 7.0 %collective-permute-done.13.refs_5_.refs_1_ = bf16[256,1536]{1,0:T(8,128)(2,1)} collective-permute-done((bf16[256,1536]{1,0:T(8,128)(2,1)}, bf16[256,1536]{1,0:T(8,128)(2,1)}, u32[]{:S(2)}, u32[]{:S(2)}) %collective-permute-start.13) | collective-permute-done | bytes 786464 | tf_op jit(solution)/shard_map/ppermute | solution.py:15
  102.9 16.0 %collective-permute-done.14.refs_6_.refs_2_ = bf16[256,1536]{1,0:T(8,128)(2,1)} collective-permute-done((bf16[256,1536]{1,0:T(8,128)(2,1)}, bf16[256,1536]{1,0:T(8,128)(2,1)}, u32[]{:S(2)}, u32[]{:S(2)}) %collective-permute-start.14) | collective-permute-done | bytes 786464 | tf_op jit(solution)/shard_map/ppermute | solution.py:15
  119.0 3.9 %collective-permute-start.19 = (bf16[256,1536]{1,0:T(8,128)(2,1)}, bf16[256,1536]{1,0:T(8,128)(2,1)}, u32[]{:S(2)}, u32[]{:S(2)}) collective-permute-start(bf16[256,1536]{1,0:T(8,128)(2,1)} %get-tuple-element.53), channel_id=1, source_target_pairs={{0,14},{2,12},{4,10},{6,8},{8,6},{10,4},{12,2},{14,0},{1,15},{3,13... | collective-permute-start | bytes 2359304 | tf_op jit(solution)/shard_map/ppermute | solution.py:15
  123.4 2.4 collective-permute-start.11
  125.8 30.0 %collective-permute-done.17.refs_9_.refs_1_ = bf16[256,1536]{1,0:T(8,128)(2,1)} collective-permute-done((bf16[256,1536]{1,0:T(8,128)(2,1)}, bf16[256,1536]{1,0:T(8,128)(2,1)}, u32[]{:S(2)}, u32[]{:S(2)}) %collective-permute-start.17) | collective-permute-done | bytes 786464 | tf_op jit(solution)/shard_map/ppermute | solution.py:15
  157.3 8.5 %collective-permute-done.18.refs_10_.refs_0_ = bf16[256,1536]{1,0:T(8,128)(2,1)} collective-permute-done((bf16[256,1536]{1,0:T(8,128)(2,1)}, bf16[256,1536]{1,0:T(8,128)(2,1)}, u32[]{:S(2)}, u32[]{:S(2)}) %collective-permute-start.18) | collective-permute-done | bytes 786464 | tf_op jit(solution)/shard_map/ppermute | solution.py:15
  165.8 2.9 collective-permute-done.19.refs_11_.refs_1_
  168.8 4.4 %collective-permute-done.12.refs_3_ = bf16[192,2048]{1,0:T(8,128)(2,1)} collective-permute-done((bf16[192,2048]{1,0:T(8,128)(2,1)}, bf16[192,2048]{1,0:T(8,128)(2,1)}, u32[]{:S(2)}, u32[]{:S(2)}) %collective-permute-start.12) | collective-permute-done | bytes 786464 | tf_op jit(solution)/shard_map/ppermute | solution.py:15
  173.1 10.1 %split_dot.2 = (f32[768,768]{1,0:T(8,128)}, f32[768,768]{1,0:T(8,128)}) custom-call(bf16[192,2048]{1,0:T(8,128)(2,1)} %get-tuple-element.42.refs_0_, bf16[192,2048]{1,0:T(8,128)(2,1)} %collective-permute-done.10.refs_1_, bf16[192,2048]{1,0:T(8,128)(2,1)} %collective-permute-done.11.refs_2_, bf16[192,2048]{1,0:T(8,128)(2,1)} %collective-permute-done.12.refs_3_, ...), custom_call_target="tpu_custom_call" | custom-call | tf_op jit(solution)/shard_map/split_dot/pallas_call | solution.py:193
  184.6 2.6 collective-permute-done.1
  187.7 4.1 %pick.3 = (bf16[192,2048]{1,0:T(8,128)(2,1)}, bf16[192,2048]{1,0:T(8,128)(2,1)}, bf16[192,2048]{1,0:T(8,128)(2,1)}, bf16[192,2048]{1,0:T(8,128)(2,1)}) custom-call(s32[1]{0:T(128)} %bitcast.12.shard_ref, s32[2,2,128]{2,1,0:T(2,128)} %pad_add_fusion.place_ref, bf16[2,2,128,256]{3,2,1,0:T(8,128)(2,1)} %join.1.refs_0_, bf16[2,2,128,256]{3,2,1,0:T(8,128)(2,1)} %copy-done.10, ...), custom_call_target="tpu_custom_call" | custom-call | tf_op jit(solution)/shard_map/pick/pallas_call | solution.py:169
  191.8 1.8 collective-permute-start.26
  195.3 17.1 %collective-permute-done.26.refs_1_ = bf16[192,2048]{1,0:T(8,128)(2,1)S(1)} collective-permute-done((bf16[192,2048]{1,0:T(8,128)(2,1)}, bf16[192,2048]{1,0:T(8,128)(2,1)S(1)}, u32[]{:S(2)}, u32[]{:S(2)}) %collective-permute-start.26) | collective-permute-done | bytes 786464 | tf_op jit(solution)/shard_map/ppermute | solution.py:15
  212.4 15.1 %collective-permute-done.27.refs_2_ = bf16[192,2048]{1,0:T(8,128)(2,1)S(1)} collective-permute-done((bf16[192,2048]{1,0:T(8,128)(2,1)}, bf16[192,2048]{1,0:T(8,128)(2,1)S(1)}, u32[]{:S(2)}, u32[]{:S(2)}) %collective-permute-start.27) | collective-permute-done | bytes 786464 | tf_op jit(solution)/shard_map/ppermute | solution.py:15
  230.7 6.9 %split_dot.3 = (f32[768,384]{1,0:T(8,128)}, f32[768,384]{1,0:T(8,128)}) custom-call(bf16[192,2048]{1,0:T(8,128)(2,1)} %get-tuple-element.61.refs_0_, bf16[192,2048]{1,0:T(8,128)(2,1)} %copy-done.5, bf16[192,2048]{1,0:T(8,128)(2,1)} %copy-done.7, bf16[192,2048]{1,0:T(8,128)(2,1)} %collective-permute-done.28.refs_3_, bf16[2048,768]{1,0:T(8,128)(2,1)} %bitcast.59), custom_call_target="tpu_custom_call" | custom-call | tf_op jit(solution)/shard_map/split_dot/pallas_call | solution.py:193
  237.6 2.7 add.77
  243.0 3.2 collective-permute-done.21.other_ref
  247.1 6.4 %row_parts.1 = (bf16[192,2048]{1,0:T(8,128)(2,1)}, bf16[192,2048]{1,0:T(8,128)(2,1)}, bf16[192,2048]{1,0:T(8,128)(2,1)}, bf16[192,2048]{1,0:T(8,128)(2,1)}) custom-call(bf16[768,384]{1,0:T(8,128)(2,1)} %copy-done.3, bf16[768,384]{1,0:T(8,128)(2,1)} %copy-done.12, bf16[2048,768]{1,0:T(8,128)(2,1)} %bitcast.60), custom_call_target="tpu_custom_call" | custom-call | tf_op jit(solution)/shard_map/row_parts/pallas_call | solution.py:206
  253.5 2.9 collective-permute-start.22
  259.5 4.4 %parts.5 = (bf16[768,256]{1,0:T(8,128)(2,1)}, bf16[768,256]{1,0:T(8,128)(2,1)}) custom-call(bf16[768,768]{1,0:T(8,128)(2,1)} %copy-done.1, bf16[768,768]{1,0:T(8,128)(2,1)} %copy-done.2, bf16[256,1536]{1,0:T(8,128)(2,1)} %collective-permute-done.18.refs_10_.refs_0_, bf16[256,1536]{1,0:T(8,128)(2,1)} %collective-permute-done.19.refs_11_.refs_1_), custom_call_target="tpu_custom_call" | custom-call | tf_op jit(solution)/shard_map/parts/pallas_call | solution.py:216
  263.9 4.4 %parts.4 = (bf16[768,256]{1,0:T(8,128)(2,1)}, bf16[768,256]{1,0:T(8,128)(2,1)}) custom-call(bf16[768,768]{1,0:T(8,128)(2,1)} %copy-done.1, bf16[768,768]{1,0:T(8,128)(2,1)} %copy-done.2, bf16[256,1536]{1,0:T(8,128)(2,1)} %collective-permute-done.16.refs_8_.refs_0_, bf16[256,1536]{1,0:T(8,128)(2,1)} %collective-permute-done.17.refs_9_.refs_1_), custom_call_target="tpu_custom_call" | custom-call | tf_op jit(solution)/shard_map/parts/pallas_call | solution.py:216
  268.3 6.7 %collective-permute-done.22.refs_1_ = bf16[192,2048]{1,0:T(8,128)(2,1)S(1)} collective-permute-done((bf16[192,2048]{1,0:T(8,128)(2,1)}, bf16[192,2048]{1,0:T(8,128)(2,1)S(1)}, u32[]{:S(2)}, u32[]{:S(2)}) %collective-permute-start.22) | collective-permute-done | bytes 786464 | tf_op jit(solution)/shard_map/ppermute | solution.py:15
  275.9 6.2 %parts.3 = (bf16[768,256]{1,0:T(8,128)(2,1)}, bf16[768,256]{1,0:T(8,128)(2,1)}, bf16[768,256]{1,0:T(8,128)(2,1)}, bf16[768,256]{1,0:T(8,128)(2,1)}) custom-call(bf16[768,768]{1,0:T(8,128)(2,1)} %copy-done.1, bf16[768,768]{1,0:T(8,128)(2,1)} %copy-done.2, bf16[256,1536]{1,0:T(8,128)(2,1)} %get-tuple-element.46.refs_4_.refs_0_, ...), custom_call_target="tpu_custom_call" | custom-call | tf_op jit(solution)/shard_map/parts/pallas_call | solution.py:216
  282.1 11.2 %collective-permute-done.23.refs_2_ = bf16[192,2048]{1,0:T(8,128)(2,1)} collective-permute-done((bf16[192,2048]{1,0:T(8,128)(2,1)}, bf16[192,2048]{1,0:T(8,128)(2,1)}, u32[]{:S(2)}, u32[]{:S(2)}) %collective-permute-start.23) | collective-permute-done | bytes 786464 | tf_op jit(solution)/shard_map/ppermute | solution.py:15
  294.9 4.0 %collective-permute-start.31 = (bf16[768,256]{1,0:T(8,128)(2,1)}, bf16[768,256]{1,0:T(8,128)(2,1)}, u32[]{:S(2)}, u32[]{:S(2)}) collective-permute-start(bf16[768,256]{1,0:T(8,128)(2,1)} %get-tuple-element.70), channel_id=1, source_target_pairs={{0,2},{2,0},{4,6},{6,4},{8,10},{10,8},{12,14},{14,12},{1,3},{3,1},... | collective-permute-start | bytes 1179656 | tf_op jit(solution)/shard_map/ppermute | solution.py:15
  298.9 6.9 %collective-permute-done.34 = bf16[768,256]{1,0:T(8,128)(2,1)S(1)} collective-permute-done((bf16[768,256]{1,0:T(8,128)(2,1)}, bf16[768,256]{1,0:T(8,128)(2,1)S(1)}, u32[]{:S(2)}, u32[]{:S(2)}) %collective-permute-start.34) | collective-permute-done | bytes 393248 | tf_op jit(solution)/shard_map/ppermute | solution.py:15
  305.8 9.1 %collective-permute-done.33 = bf16[768,256]{1,0:T(8,128)(2,1)S(1)} collective-permute-done((bf16[768,256]{1,0:T(8,128)(2,1)}, bf16[768,256]{1,0:T(8,128)(2,1)S(1)}, u32[]{:S(2)}, u32[]{:S(2)}) %collective-permute-start.33) | collective-permute-done | bytes 393248 | tf_op jit(solution)/shard_map/ppermute | solution.py:15
  316.4 4.1 %combine.1 = bf16[8,2,128,256]{3,2,1,0:T(8,128)(2,1)} custom-call(s32[2,2,128]{2,1,0:T(2,128)} %pad_add_fusion.place_ref, f32[2,2,128]{2,1,0:T(2,128)} %pad_maximum_fusion.3.mix_ref.refs_8_, bf16[192,2048]{1,0:T(8,128)(2,1)} %get-tuple-element.57.refs_0_, bf16[192,2048]{1,0:T(8,128)(2,1)} %copy-done.11, bf16[192,2048]{1,0:T(8,128)(2,1)} %collective-permute-done.23.refs_2_, ...), custom_call_target="tpu_custom_call" | custom-call | tf_op jit(solution)/shard_map/combine/pallas_call | solution.py:241
  320.5 3.6 all-to-all-start.1
  324.1 2.2 add_convert_fusion
  327.5 4.8 %collective-permute-start.39 = (bf16[2,96,256]{2,1,0:T(8,128)(2,1)S(1)}, bf16[2,96,256]{2,1,0:T(8,128)(2,1)S(1)}, u32[]{:S(2)}, u32[]{:S(2)}) collective-permute-start(bf16[2,96,256]{2,1,0:T(8,128)(2,1)S(1)} %bitcast.70), channel_id=1, source_target_pairs={{0,32},{16,48},{32,0},{48,16},{1,33},{17,49},{33,1},{49,17},{2,34}... | collective-permute-start | bytes 294920 | tf_op jit(solution)/shard_map/ppermute | solution.py:15
  334.9 3.2 collective-permute-start.38
  338.1 7.6 %weight_grad.3 = bf16[1,4096,384]{2,1,0:T(8,128)(2,1)} custom-call(s32[1]{0:T(128)} %bitcast.12.shard_ref, bf16[192,2048]{1,0:T(8,128)(2,1)} %get-tuple-element.61.refs_0_, bf16[192,2048]{1,0:T(8,128)(2,1)} %copy-done.5, bf16[192,2048]{1,0:T(8,128)(2,1)} %copy-done.7, bf16[192,2048]{1,0:T(8,128)(2,1)} %collective-permute-done.28.refs_3_, ...), custom_call_target="tpu_custom_call" | custom-call | flops 2415919104 | bytes 10027008 | tf_op jit(solution)/shard_map/weight_grad/pallas_call | solution.py:116
  349.7 9.7 %weight_grad.2 = (bf16[1,4096,384]{2,1,0:T(8,128)(2,1)}, bf16[1,4096,384]{2,1,0:T(8,128)(2,1)}) custom-call(s32[1]{0:T(128)} %bitcast.12.shard_ref, bf16[192,2048]{1,0:T(8,128)(2,1)} %get-tuple-element.42.refs_0_, bf16[192,2048]{1,0:T(8,128)(2,1)} %collective-permute-done.10.refs_1_, bf16[192,2048]{1,0:T(8,128)(2,1)} %collective-permute-done.11.refs_2_, ...), custom_call_target="tpu_custom_call" | custom-call | flops 4831838208 | bytes 13762560 | tf_op jit(solution)/shard_map/weight_grad/pallas_call | solution.py:116
  360.0 1.9 finish.1
  (155 shorter events, 39.4 us)
Async XLA Ops:
  1.5 13.5 %collective-permute-start.2 = (bf16[2,128,256]{2,1,0:T(8,128)(2,1)S(1)}, bf16[2,128,256]{2,1,0:T(8,128)(2,1)S(1)}, u32[]{:S(2)}, u32[]{:S(2)}) collective-permute-start(bf16[2,128,256]{2,1,0:T(8,128)(2,1)S(1)} %pad_maximum_fusion.2), channel_id=1, source_target_pairs={{0,64},{64,0},{1,65},{65,1},{2,66},{66,2},{3,67},{67,3},{4,68},{68... | collective-permute-start | bytes 393224 | tf_op jit(solution)/shard_map/ppermute | solution.py:15
  3.5 23.1 %collective-permute-start = (s32[128,2]{0,1:T(2,128)}, s32[128,2]{0,1:T(2,128)S(1)}, u32[]{:S(2)}, u32[]{:S(2)}) collective-permute-start(s32[128,2]{0,1:T(2,128)} %param.8), channel_id=1, source_target_pairs={{0,64},{64,0},{1,65},{65,1},{2,66},{66,2},{3,67},{67,3},{4,68},{68... | collective-permute-start | bytes 3080 | tf_op jit(solution)/shard_map/ppermute | solution.py:15
  6.8 222.2 %all-to-all-start = ((bf16[8,256,768]{2,1,0:T(8,128)(2,1)}), bf16[8,256,768]{2,1,0:T(8,128)(2,1)S(1)}, u32[]{:S(2)}, u32[]{:S(2)}) async-start(bf16[8,256,768]{2,1,0:T(8,128)(2,1)} %pack.3), calls=%async_computation | async-start | bytes 6291456 | tf_op jit(solution)/shard_map/all_to_all | solution.py:86
  17.4 47.9 %collective-permute-start.3 = (bf16[2,2,128,256]{3,2,1,0:T(8,128)(2,1)}, bf16[2,2,128,256]{3,2,1,0:T(8,128)(2,1)S(1)}, u32[]{:S(2)}, u32[]{:S(2)}) collective-permute-start(bf16[2,2,128,256]{3,2,1,0:T(8,128)(2,1)} %join.1.refs_0_), channel_id=1, source_target_pairs={{0,2},{2,0},{4,6},{6,4},{8,10},{10,8},{12,14},{14,12},{1,3},{3,1},... | collective-permute-start | bytes 786440 | tf_op jit(solution)/shard_map/ppermute | solution.py:15
  19.4 50.8 %collective-permute-start.4 = (bf16[2,2,128,256]{3,2,1,0:T(8,128)(2,1)}, bf16[2,2,128,256]{3,2,1,0:T(8,128)(2,1)}, u32[]{:S(2)}, u32[]{:S(2)}) collective-permute-start(bf16[2,2,128,256]{3,2,1,0:T(8,128)(2,1)} %join.1.refs_0_), channel_id=1, source_target_pairs={{0,4},{2,6},{4,0},{6,2},{8,12},{10,14},{12,8},{14,10},{1,5},{3,7},... | collective-permute-start | bytes 786440 | tf_op jit(solution)/shard_map/ppermute | solution.py:15
  23.0 59.0 %collective-permute-start.5 = (bf16[2,2,128,256]{3,2,1,0:T(8,128)(2,1)}, bf16[2,2,128,256]{3,2,1,0:T(8,128)(2,1)}, u32[]{:S(2)}, u32[]{:S(2)}) collective-permute-start(bf16[2,2,128,256]{3,2,1,0:T(8,128)(2,1)} %join.1.refs_0_), channel_id=1, source_target_pairs={{0,6},{2,4},{4,2},{6,0},{8,14},{10,12},{12,10},{14,8},{1,7},{3,5},... | collective-permute-start | bytes 786440 | tf_op jit(solution)/shard_map/ppermute | solution.py:15
  23.1 59.1 %collective-permute-start.6 = (bf16[2,2,128,256]{3,2,1,0:T(8,128)(2,1)}, bf16[2,2,128,256]{3,2,1,0:T(8,128)(2,1)}, u32[]{:S(2)}, u32[]{:S(2)}) collective-permute-start(bf16[2,2,128,256]{3,2,1,0:T(8,128)(2,1)} %join.1.refs_0_), channel_id=1, source_target_pairs={{0,8},{2,10},{4,12},{6,14},{8,0},{10,2},{12,4},{14,6},{1,9},{3,11}... | collective-permute-start | bytes 786440 | tf_op jit(solution)/shard_map/ppermute | solution.py:15
  26.6 56.7 %collective-permute-start.7 = (bf16[2,2,128,256]{3,2,1,0:T(8,128)(2,1)}, bf16[2,2,128,256]{3,2,1,0:T(8,128)(2,1)}, u32[]{:S(2)}, u32[]{:S(2)}) collective-permute-start(bf16[2,2,128,256]{3,2,1,0:T(8,128)(2,1)} %join.1.refs_0_), channel_id=1, source_target_pairs={{0,10},{2,8},{4,14},{6,12},{8,2},{10,0},{12,6},{14,4},{1,11},{3,9}... | collective-permute-start | bytes 786440 | tf_op jit(solution)/shard_map/ppermute | solution.py:15
  65.3 21.6 %collective-permute-start.8 = (bf16[2,2,128,256]{3,2,1,0:T(8,128)(2,1)}, bf16[2,2,128,256]{3,2,1,0:T(8,128)(2,1)}, u32[]{:S(2)}, u32[]{:S(2)}) collective-permute-start(bf16[2,2,128,256]{3,2,1,0:T(8,128)(2,1)} %join.1.refs_0_), channel_id=1, source_target_pairs={{0,12},{2,14},{4,8},{6,10},{8,4},{10,6},{12,0},{14,2},{1,13},{3,15... | collective-permute-start | bytes 786440 | tf_op jit(solution)/shard_map/ppermute | solution.py:15
  70.2 19.7 %collective-permute-start.9 = (bf16[2,2,128,256]{3,2,1,0:T(8,128)(2,1)}, bf16[2,2,128,256]{3,2,1,0:T(8,128)(2,1)}, u32[]{:S(2)}, u32[]{:S(2)}) collective-permute-start(bf16[2,2,128,256]{3,2,1,0:T(8,128)(2,1)} %join.1.refs_0_), channel_id=1, source_target_pairs={{0,14},{2,12},{4,10},{6,8},{8,6},{10,4},{12,2},{14,0},{1,15},{3,13... | collective-permute-start | bytes 786440 | tf_op jit(solution)/shard_map/ppermute | solution.py:15
  82.1 20.8 %collective-permute-start.13 = (bf16[256,1536]{1,0:T(8,128)(2,1)}, bf16[256,1536]{1,0:T(8,128)(2,1)}, u32[]{:S(2)}, u32[]{:S(2)}) collective-permute-start(bf16[256,1536]{1,0:T(8,128)(2,1)} %get-tuple-element.47), channel_id=1, source_target_pairs={{0,2},{2,0},{4,6},{6,4},{8,10},{10,8},{12,14},{14,12},{1,3},{3,1},... | collective-permute-start | bytes 2359304 | tf_op jit(solution)/shard_map/ppermute | solution.py:15
  82.2 36.8 %collective-permute-start.14 = (bf16[256,1536]{1,0:T(8,128)(2,1)}, bf16[256,1536]{1,0:T(8,128)(2,1)}, u32[]{:S(2)}, u32[]{:S(2)}) collective-permute-start(bf16[256,1536]{1,0:T(8,128)(2,1)} %get-tuple-element.48), channel_id=1, source_target_pairs={{0,4},{2,6},{4,0},{6,2},{8,12},{10,14},{12,8},{14,10},{1,5},{3,7},... | collective-permute-start | bytes 2359304 | tf_op jit(solution)/shard_map/ppermute | solution.py:15
  83.4 39.5 %collective-permute-start.15 = (bf16[256,1536]{1,0:T(8,128)(2,1)}, bf16[256,1536]{1,0:T(8,128)(2,1)}, u32[]{:S(2)}, u32[]{:S(2)}) collective-permute-start(bf16[256,1536]{1,0:T(8,128)(2,1)} %get-tuple-element.49), channel_id=1, source_target_pairs={{0,6},{2,4},{4,2},{6,0},{8,14},{10,12},{12,10},{14,8},{1,7},{3,5},... | collective-permute-start | bytes 2359304 | tf_op jit(solution)/shard_map/ppermute | solution.py:15
  86.9 36.5 %collective-permute-start.16 = (bf16[256,1536]{1,0:T(8,128)(2,1)}, bf16[256,1536]{1,0:T(8,128)(2,1)}, u32[]{:S(2)}, u32[]{:S(2)}) collective-permute-start(bf16[256,1536]{1,0:T(8,128)(2,1)} %get-tuple-element.50), channel_id=1, source_target_pairs={{0,8},{2,10},{4,12},{6,14},{8,0},{10,2},{12,4},{14,6},{1,9},{3,11}... | collective-permute-start | bytes 2359304 | tf_op jit(solution)/shard_map/ppermute | solution.py:15
  89.9 65.9 %collective-permute-start.17 = (bf16[256,1536]{1,0:T(8,128)(2,1)}, bf16[256,1536]{1,0:T(8,128)(2,1)}, u32[]{:S(2)}, u32[]{:S(2)}) collective-permute-start(bf16[256,1536]{1,0:T(8,128)(2,1)} %get-tuple-element.51), channel_id=1, source_target_pairs={{0,10},{2,8},{4,14},{6,12},{8,2},{10,0},{12,6},{14,4},{1,11},{3,9}... | collective-permute-start | bytes 2359304 | tf_op jit(solution)/shard_map/ppermute | solution.py:15
  102.9 62.9 %collective-permute-start.18 = (bf16[256,1536]{1,0:T(8,128)(2,1)}, bf16[256,1536]{1,0:T(8,128)(2,1)}, u32[]{:S(2)}, u32[]{:S(2)}) collective-permute-start(bf16[256,1536]{1,0:T(8,128)(2,1)} %get-tuple-element.52), channel_id=1, source_target_pairs={{0,12},{2,14},{4,8},{6,10},{8,4},{10,6},{12,0},{14,2},{1,13},{3,15... | collective-permute-start | bytes 2359304 | tf_op jit(solution)/shard_map/ppermute | solution.py:15
  119.0 49.8 %collective-permute-start.19 = (bf16[256,1536]{1,0:T(8,128)(2,1)}, bf16[256,1536]{1,0:T(8,128)(2,1)}, u32[]{:S(2)}, u32[]{:S(2)}) collective-permute-start(bf16[256,1536]{1,0:T(8,128)(2,1)} %get-tuple-element.53), channel_id=1, source_target_pairs={{0,14},{2,12},{4,10},{6,8},{8,6},{10,4},{12,2},{14,0},{1,15},{3,13... | collective-permute-start | bytes 2359304 | tf_op jit(solution)/shard_map/ppermute | solution.py:15
  122.8 45.9 %collective-permute-start.10 = (bf16[192,2048]{1,0:T(8,128)(2,1)}, bf16[192,2048]{1,0:T(8,128)(2,1)}, u32[]{:S(2)}, u32[]{:S(2)}) collective-permute-start(bf16[192,2048]{1,0:T(8,128)(2,1)} %get-tuple-element.43), channel_id=1, source_target_pairs={{0,16},{16,0},{32,48},{48,32},{1,17},{17,1},{33,49},{49,33},{2,18}... | collective-permute-start | bytes 2359304 | tf_op jit(solution)/shard_map/ppermute | solution.py:15
  123.4 45.4 %collective-permute-start.11 = (bf16[192,2048]{1,0:T(8,128)(2,1)}, bf16[192,2048]{1,0:T(8,128)(2,1)}, u32[]{:S(2)}, u32[]{:S(2)}) collective-permute-start(bf16[192,2048]{1,0:T(8,128)(2,1)} %get-tuple-element.44), channel_id=1, source_target_pairs={{0,32},{16,48},{32,0},{48,16},{1,33},{17,49},{33,1},{49,17},{2,34}... | collective-permute-start | bytes 2359304 | tf_op jit(solution)/shard_map/ppermute | solution.py:15
  155.8 17.3 %collective-permute-start.12 = (bf16[192,2048]{1,0:T(8,128)(2,1)}, bf16[192,2048]{1,0:T(8,128)(2,1)}, u32[]{:S(2)}, u32[]{:S(2)}) collective-permute-start(bf16[192,2048]{1,0:T(8,128)(2,1)} %get-tuple-element.45), channel_id=1, source_target_pairs={{0,48},{16,32},{32,16},{48,0},{1,49},{17,33},{33,17},{49,1},{2,50}... | collective-permute-start | bytes 2359304 | tf_op jit(solution)/shard_map/ppermute | solution.py:15
  183.3 54.3 %collective-permute-start.20 = (f32[768,768]{1,0:T(8,128)}, f32[768,768]{1,0:T(8,128)}, u32[]{:S(2)}, u32[]{:S(2)}) collective-permute-start(f32[768,768]{1,0:T(8,128)} %get-tuple-element.55), channel_id=1, source_target_pairs={{0,1},{1,0},{2,3},{3,2},{4,5},{5,4},{6,7},{7,6},{8,9},{9,8},{10,11... | collective-permute-start | bytes 7077896 | tf_op jit(solution)/shard_map/ppermute | solution.py:15
  191.8 20.6 %collective-permute-start.26 = (bf16[192,2048]{1,0:T(8,128)(2,1)}, bf16[192,2048]{1,0:T(8,128)(2,1)S(1)}, u32[]{:S(2)}, u32[]{:S(2)}) collective-permute-start(bf16[192,2048]{1,0:T(8,128)(2,1)} %get-tuple-element.62), channel_id=1, source_target_pairs={{0,16},{16,0},{32,48},{48,32},{1,17},{17,1},{33,49},{49,33},{2,18}... | collective-permute-start | bytes 2359304 | tf_op jit(solution)/shard_map/ppermute | solution.py:15
  193.6 33.9 %collective-permute-start.27 = (bf16[192,2048]{1,0:T(8,128)(2,1)}, bf16[192,2048]{1,0:T(8,128)(2,1)S(1)}, u32[]{:S(2)}, u32[]{:S(2)}) collective-permute-start(bf16[192,2048]{1,0:T(8,128)(2,1)} %get-tuple-element.63), channel_id=1, source_target_pairs={{0,32},{16,48},{32,0},{48,16},{1,33},{17,49},{33,1},{49,17},{2,34}... | collective-permute-start | bytes 2359304 | tf_op jit(solution)/shard_map/ppermute | solution.py:15
  193.8 35.2 %collective-permute-start.28 = (bf16[192,2048]{1,0:T(8,128)(2,1)}, bf16[192,2048]{1,0:T(8,128)(2,1)}, u32[]{:S(2)}, u32[]{:S(2)}) collective-permute-start(bf16[192,2048]{1,0:T(8,128)(2,1)} %get-tuple-element.64), channel_id=1, source_target_pairs={{0,48},{16,32},{32,16},{48,0},{1,49},{17,33},{33,17},{49,1},{2,50}... | collective-permute-start | bytes 2359304 | tf_op jit(solution)/shard_map/ppermute | solution.py:15
  242.3 16.2 %collective-permute-start.30 = (bf16[768,768]{1,0:T(8,128)(2,1)S(1)}, bf16[768,768]{1,0:T(8,128)(2,1)S(1)}, u32[]{:S(2)}, u32[]{:S(2)}) collective-permute-start(bf16[768,768]{1,0:T(8,128)(2,1)S(1)} %pad_maximum_fusion.own_ref.refs_8_), channel_id=1, source_target_pairs={{0,1},{1,0},{2,3},{3,2},{4,5},{5,4},{6,7},{7,6},{8,9},{9,8},{10,11... | collective-permute-start | bytes 3538952 | tf_op jit(solution)/shard_map/ppermute | solution.py:15
  253.5 21.5 %collective-permute-start.22 = (bf16[192,2048]{1,0:T(8,128)(2,1)}, bf16[192,2048]{1,0:T(8,128)(2,1)S(1)}, u32[]{:S(2)}, u32[]{:S(2)}) collective-permute-start(bf16[192,2048]{1,0:T(8,128)(2,1)} %get-tuple-element.58), channel_id=1, source_target_pairs={{0,16},{16,0},{32,48},{48,32},{1,17},{17,1},{33,49},{49,33},{2,18}... | collective-permute-start | bytes 2359304 | tf_op jit(solution)/shard_map/ppermute | solution.py:15
  256.4 36.9 %collective-permute-start.23 = (bf16[192,2048]{1,0:T(8,128)(2,1)}, bf16[192,2048]{1,0:T(8,128)(2,1)}, u32[]{:S(2)}, u32[]{:S(2)}) collective-permute-start(bf16[192,2048]{1,0:T(8,128)(2,1)} %get-tuple-element.59), channel_id=1, source_target_pairs={{0,32},{16,48},{32,0},{48,16},{1,33},{17,49},{33,1},{49,17},{2,34}... | collective-permute-start | bytes 2359304 | tf_op jit(solution)/shard_map/ppermute | solution.py:15
  258.0 36.7 %collective-permute-start.24 = (bf16[192,2048]{1,0:T(8,128)(2,1)}, bf16[192,2048]{1,0:T(8,128)(2,1)}, u32[]{:S(2)}, u32[]{:S(2)}) collective-permute-start(bf16[192,2048]{1,0:T(8,128)(2,1)} %get-tuple-element.60), channel_id=1, source_target_pairs={{0,48},{16,32},{32,16},{48,0},{1,49},{17,33},{33,17},{49,1},{2,50}... | collective-permute-start | bytes 2359304 | tf_op jit(solution)/shard_map/ppermute | solution.py:15
  263.9 30.8 %collective-permute-start.37 = (bf16[768,256]{1,0:T(8,128)(2,1)}, bf16[768,256]{1,0:T(8,128)(2,1)S(1)}, u32[]{:S(2)}, u32[]{:S(2)}) collective-permute-start(bf16[768,256]{1,0:T(8,128)(2,1)} %get-tuple-element.76), channel_id=1, source_target_pairs={{0,14},{2,12},{4,10},{6,8},{8,6},{10,4},{12,2},{14,0},{1,15},{3,13... | collective-permute-start | bytes 1179656 | tf_op jit(solution)/shard_map/ppermute | solution.py:15
  263.9 30.9 %collective-permute-start.36 = (bf16[768,256]{1,0:T(8,128)(2,1)}, bf16[768,256]{1,0:T(8,128)(2,1)S(1)}, u32[]{:S(2)}, u32[]{:S(2)}) collective-permute-start(bf16[768,256]{1,0:T(8,128)(2,1)} %get-tuple-element.75), channel_id=1, source_target_pairs={{0,12},{2,14},{4,8},{6,10},{8,4},{10,6},{12,0},{14,2},{1,13},{3,15... | collective-permute-start | bytes 1179656 | tf_op jit(solution)/shard_map/ppermute | solution.py:15
  275.9 22.9 %collective-permute-start.35 = (bf16[768,256]{1,0:T(8,128)(2,1)}, bf16[768,256]{1,0:T(8,128)(2,1)}, u32[]{:S(2)}, u32[]{:S(2)}) collective-permute-start(bf16[768,256]{1,0:T(8,128)(2,1)} %get-tuple-element.74), channel_id=1, source_target_pairs={{0,10},{2,8},{4,14},{6,12},{8,2},{10,0},{12,6},{14,4},{1,11},{3,9}... | collective-permute-start | bytes 1179656 | tf_op jit(solution)/shard_map/ppermute | solution.py:15
  293.3 12.5 %collective-permute-start.34 = (bf16[768,256]{1,0:T(8,128)(2,1)}, bf16[768,256]{1,0:T(8,128)(2,1)S(1)}, u32[]{:S(2)}, u32[]{:S(2)}) collective-permute-start(bf16[768,256]{1,0:T(8,128)(2,1)} %get-tuple-element.73), channel_id=1, source_target_pairs={{0,8},{2,10},{4,12},{6,14},{8,0},{10,2},{12,4},{14,6},{1,9},{3,11}... | collective-permute-start | bytes 1179656 | tf_op jit(solution)/shard_map/ppermute | solution.py:15
  294.7 20.1 %collective-permute-start.33 = (bf16[768,256]{1,0:T(8,128)(2,1)}, bf16[768,256]{1,0:T(8,128)(2,1)S(1)}, u32[]{:S(2)}, u32[]{:S(2)}) collective-permute-start(bf16[768,256]{1,0:T(8,128)(2,1)} %get-tuple-element.72), channel_id=1, source_target_pairs={{0,6},{2,4},{4,2},{6,0},{8,14},{10,12},{12,10},{14,8},{1,7},{3,5},... | collective-permute-start | bytes 1179656 | tf_op jit(solution)/shard_map/ppermute | solution.py:15
  294.8 20.1 %collective-permute-start.32 = (bf16[768,256]{1,0:T(8,128)(2,1)}, bf16[768,256]{1,0:T(8,128)(2,1)S(1)}, u32[]{:S(2)}, u32[]{:S(2)}) collective-permute-start(bf16[768,256]{1,0:T(8,128)(2,1)} %get-tuple-element.71), channel_id=1, source_target_pairs={{0,4},{2,6},{4,0},{6,2},{8,12},{10,14},{12,8},{14,10},{1,5},{3,7},... | collective-permute-start | bytes 1179656 | tf_op jit(solution)/shard_map/ppermute | solution.py:15
  294.9 29.3 %collective-permute-start.31 = (bf16[768,256]{1,0:T(8,128)(2,1)}, bf16[768,256]{1,0:T(8,128)(2,1)}, u32[]{:S(2)}, u32[]{:S(2)}) collective-permute-start(bf16[768,256]{1,0:T(8,128)(2,1)} %get-tuple-element.70), channel_id=1, source_target_pairs={{0,2},{2,0},{4,6},{6,4},{8,10},{10,8},{12,14},{14,12},{1,3},{3,1},... | collective-permute-start | bytes 1179656 | tf_op jit(solution)/shard_map/ppermute | solution.py:15
  298.9 28.6 %collective-permute-start.46 = (bf16[192,2048]{1,0:T(8,128)(2,1)S(1)}, bf16[192,2048]{1,0:T(8,128)(2,1)}, u32[]{:S(2)}, u32[]{:S(2)}) collective-permute-start(bf16[192,2048]{1,0:T(8,128)(2,1)S(1)} %copy-done.4), channel_id=1, source_target_pairs={{0,1},{1,0},{2,3},{3,2},{4,5},{5,4},{6,7},{7,6},{8,9},{9,8},{10,11... | collective-permute-start | bytes 2359304 | tf_op jit(solution)/shard_map/ppermute | solution.py:15
  305.8 26.5 %collective-permute-start.47 = (bf16[192,2048]{1,0:T(8,128)(2,1)S(1)}, bf16[192,2048]{1,0:T(8,128)(2,1)}, u32[]{:S(2)}, u32[]{:S(2)}) collective-permute-start(bf16[192,2048]{1,0:T(8,128)(2,1)S(1)} %copy-done.6), channel_id=1, source_target_pairs={{0,1},{1,0},{2,3},{3,2},{4,5},{5,4},{6,7},{7,6},{8,9},{9,8},{10,11... | collective-permute-start | bytes 2359304 | tf_op jit(solution)/shard_map/ppermute | solution.py:15
  314.9 17.4 %collective-permute-start.48 = (bf16[192,2048]{1,0:T(8,128)(2,1)S(1)}, bf16[192,2048]{1,0:T(8,128)(2,1)}, u32[]{:S(2)}, u32[]{:S(2)}) collective-permute-start(bf16[192,2048]{1,0:T(8,128)(2,1)S(1)} %copy-done.8), channel_id=1, source_target_pairs={{0,1},{1,0},{2,3},{3,2},{4,5},{5,4},{6,7},{7,6},{8,9},{9,8},{10,11... | collective-permute-start | bytes 2359304 | tf_op jit(solution)/shard_map/ppermute | solution.py:15
  315.6 17.2 %collective-permute-start.49 = (bf16[192,2048]{1,0:T(8,128)(2,1)}, bf16[192,2048]{1,0:T(8,128)(2,1)}, u32[]{:S(2)}, u32[]{:S(2)}) collective-permute-start(bf16[192,2048]{1,0:T(8,128)(2,1)} %collective-permute-done.28.refs_3_), channel_id=1, source_target_pairs={{0,1},{1,0},{2,3},{3,2},{4,5},{5,4},{6,7},{7,6},{8,9},{9,8},{10,11... | collective-permute-start | bytes 2359304 | tf_op jit(solution)/shard_map/ppermute | solution.py:15
  320.5 27.9 %all-to-all-start.1 = ((bf16[8,2,128,256]{3,2,1,0:T(8,128)(2,1)}), bf16[8,2,128,256]{3,2,1,0:T(8,128)(2,1)S(1)}, u32[]{:S(2)}, u32[]{:S(2)}) async-start(bf16[8,2,128,256]{3,2,1,0:T(8,128)(2,1)} %combine.1), calls=%async_computation.1 | async-start | bytes 2097152 | tf_op jit(solution)/shard_map/all_to_all | solution.py:86
  327.5 7.4 %collective-permute-start.39 = (bf16[2,96,256]{2,1,0:T(8,128)(2,1)S(1)}, bf16[2,96,256]{2,1,0:T(8,128)(2,1)S(1)}, u32[]{:S(2)}, u32[]{:S(2)}) collective-permute-start(bf16[2,96,256]{2,1,0:T(8,128)(2,1)S(1)} %bitcast.70), channel_id=1, source_target_pairs={{0,32},{16,48},{32,0},{48,16},{1,33},{17,49},{33,1},{49,17},{2,34}... | collective-permute-start | bytes 294920 | tf_op jit(solution)/shard_map/ppermute | solution.py:15
  332.3 16.3 %collective-permute-start.42 = (bf16[192,2048]{1,0:T(8,128)(2,1)}, bf16[192,2048]{1,0:T(8,128)(2,1)S(1)}, u32[]{:S(2)}, u32[]{:S(2)}) collective-permute-start(bf16[192,2048]{1,0:T(8,128)(2,1)} %get-tuple-element.42.refs_0_), channel_id=1, source_target_pairs={{0,1},{1,0},{2,3},{3,2},{4,5},{5,4},{6,7},{7,6},{8,9},{9,8},{10,11... | collective-permute-start | bytes 2359304 | tf_op jit(solution)/shard_map/ppermute | solution.py:15
  332.3 17.4 %collective-permute-start.43 = (bf16[192,2048]{1,0:T(8,128)(2,1)}, bf16[192,2048]{1,0:T(8,128)(2,1)}, u32[]{:S(2)}, u32[]{:S(2)}) collective-permute-start(bf16[192,2048]{1,0:T(8,128)(2,1)} %collective-permute-done.10.refs_1_), channel_id=1, source_target_pairs={{0,1},{1,0},{2,3},{3,2},{4,5},{5,4},{6,7},{7,6},{8,9},{9,8},{10,11... | collective-permute-start | bytes 2359304 | tf_op jit(solution)/shard_map/ppermute | solution.py:15
  332.8 16.9 %collective-permute-start.44 = (bf16[192,2048]{1,0:T(8,128)(2,1)}, bf16[192,2048]{1,0:T(8,128)(2,1)}, u32[]{:S(2)}, u32[]{:S(2)}) collective-permute-start(bf16[192,2048]{1,0:T(8,128)(2,1)} %collective-permute-done.11.refs_2_), channel_id=1, source_target_pairs={{0,1},{1,0},{2,3},{3,2},{4,5},{5,4},{6,7},{7,6},{8,9},{9,8},{10,11... | collective-permute-start | bytes 2359304 | tf_op jit(solution)/shard_map/ppermute | solution.py:15
  332.9 16.8 %collective-permute-start.45 = (bf16[192,2048]{1,0:T(8,128)(2,1)}, bf16[192,2048]{1,0:T(8,128)(2,1)}, u32[]{:S(2)}, u32[]{:S(2)}) collective-permute-start(bf16[192,2048]{1,0:T(8,128)(2,1)} %collective-permute-done.12.refs_3_), channel_id=1, source_target_pairs={{0,1},{1,0},{2,3},{3,2},{4,5},{5,4},{6,7},{7,6},{8,9},{9,8},{10,11... | collective-permute-start | bytes 2359304 | tf_op jit(solution)/shard_map/ppermute | solution.py:15
  334.9 10.9 %collective-permute-start.38 = (bf16[2,96,256]{2,1,0:T(8,128)(2,1)}, bf16[2,96,256]{2,1,0:T(8,128)(2,1)S(1)}, u32[]{:S(2)}, u32[]{:S(2)}) collective-permute-start(bf16[2,96,256]{2,1,0:T(8,128)(2,1)} %bitcast.23), channel_id=1, source_target_pairs={{0,16},{16,0},{32,48},{48,32},{1,17},{17,1},{33,49},{49,33},{2,18}... | collective-permute-start | bytes 294920 | tf_op jit(solution)/shard_map/ppermute | solution.py:15
  347.4 12.0 %collective-permute-start.41 = (bf16[4,96,256]{2,1,0:T(8,128)(2,1)S(1)}, bf16[4,96,256]{2,1,0:T(8,128)(2,1)S(1)}, u32[]{:S(2)}, u32[]{:S(2)}) collective-permute-start(bf16[4,96,256]{2,1,0:T(8,128)(2,1)S(1)} %get-tuple-element.86), channel_id=1, source_target_pairs={{0,64},{64,0},{1,65},{65,1},{2,66},{66,2},{3,67},{67,3},{4,68},{68... | collective-permute-start | bytes 589832 | tf_op jit(solution)/shard_map/ppermute | solution.py:15
  348.6 13.4 %collective-permute-start.25 = (bf16[128,256]{1,0:T(8,128)(2,1)S(1)}, bf16[128,256]{1,0:T(8,128)(2,1)S(1)}, u32[]{:S(2)}, u32[]{:S(2)}) collective-permute-start(bf16[128,256]{1,0:T(8,128)(2,1)S(1)} %fusion.2), channel_id=1, source_target_pairs={{0,64},{64,0},{1,65},{65,1},{2,66},{66,2},{3,67},{67,3},{4,68},{68... | collective-permute-start | bytes 196616 | tf_op jit(solution)/shard_map/ppermute | solution.py:15
  (27 other events, 241.5 us)
